TPU v7x, 32 devices: a whole 2x2x4 slice. The times are simulated.
32 devices in a mesh: tm: 2 (over x), space: 16 (over z, y, core).
Axes of the slice: x: 2, y: 2, z: 4, core: 2. Of those that a mesh axis runs over, the one named last changes fastest.
Arguments:
- start_state: float32 [2, 2, 1024, 1024], P('tm', None, 'space'), may hold values from -6 to 6
- rigidity: float32 [1024, 1024], P('space'), may hold values from 0.5 to 2
- inv_mass: float32 [1024, 1024], P('space'), may hold values from 0.5 to 2
- gust_load: float32 [1024, 1024], P('space'), may hold values from -6 to 6
- kl_coeff: float32 [4, 4], replicated, may hold values from -3 to 3
- gust_history: float32 [8], P('tm'), may hold values from -4 to 4
Outputs:
- end_state: float32 [2, 2, 1024, 1024], P('tm', None, 'space')
All inputs are finite; a program needn't handle non-finite values.
Results may differ from a plain program's by a relative error of at most 0.000082.
Values sent between devices are 32-bit elements; how exact they have to be, the bound alone decides.
No kernel may reach another device: no remote copies, remote signals or barrier semaphores. Data moves between devices by JAX's collectives and lax.ppermute only.
A program may use at most 64 MiB of HBM per device.

v0:
```python
import jax
import jax.numpy as jnp
from jax import lax
from jax.sharding import PartitionSpec as P

FINE = 4
ITERS = 2
KL = 4


STIFF_SCALE = 1.0 / 64.0
TIME_STEP = 0.18
HALF_STEP = 0.09
DAMPING = 0.05


def extended(block, sides, width):
    for axis, dim in sides:
        count = lax.axis_size(axis)
        forward = [(i, i + 1) for i in range(count - 1)]
        backward = [(target, source) for source, target in forward]
        low = lax.ppermute(
            lax.slice_in_dim(block, block.shape[dim] - width, None, axis=dim), axis, forward
        )
        high = lax.ppermute(lax.slice_in_dim(block, 0, width, axis=dim), axis, backward)
        block = jnp.concatenate([low, block, high], axis=dim)
    return block


def passed_along(block, axis, distance):
    devices = range(lax.axis_size(axis))
    route = [(i - distance, i) for i in devices if i - distance in devices]
    return lax.ppermute(block, axis, route)


def laplace(padded):
    return (
        padded[2:, 1:-1]
        + padded[:-2, 1:-1]
        + padded[1:-1, 2:]
        + padded[1:-1, :-2]
        - 4.0 * padded[1:-1, 1:-1]
    )


def mode_table(positions, extent):
    orders = (jnp.arange(KL) + 1).astype(jnp.float32)
    coords = (positions.astype(jnp.float32) + 0.5) / extent
    return jnp.cos(jnp.pi * orders[:, None] * coords[None, :])


def build_rigidity(rigidity, kl_coeff, first_row, extent_rows, extent_cols):
    row_count = rigidity.shape[0]
    col_count = rigidity.shape[1]
    across = mode_table(first_row + jnp.arange(row_count), extent_rows)
    along_chord = mode_table(jnp.arange(col_count), extent_cols)
    mixed = jnp.dot(kl_coeff, along_chord, precision=lax.Precision.HIGHEST)
    kl_field = jnp.dot(across.T, mixed, precision=lax.Precision.HIGHEST)
    return rigidity * jnp.exp(0.5 * jnp.tanh(kl_field))


def apply_padded(widened, rigid_rim):
    weighted = rigid_rim * laplace(jnp.pad(widened, ((0, 0), (1, 1))))
    return STIFF_SCALE * laplace(jnp.pad(weighted, ((0, 0), (1, 1))))


def crop_rows(values_in, have_rim, want_rim):
    margin = have_rim - want_rim
    return values_in[margin : values_in.shape[0] - margin]


def accelerate(velocity, stiff_now, inv_mass, gust_load, gust_value):
    return inv_mass * (gust_load * gust_value - stiff_now) - DAMPING * velocity


def coarse_step(position, velocity, stiff_now, inv_mass, gust_load, gust_value):
    coarse_span = FINE * TIME_STEP
    new_vel = velocity + coarse_span * accelerate(
        velocity, stiff_now, inv_mass, gust_load, gust_value
    )
    return (position + coarse_span * new_vel, new_vel)


def per_device(start_state, rigidity, inv_mass, gust_load, kl_coeff, gust_history):
    row_count = rigidity.shape[0]
    col_count = rigidity.shape[1]
    space_count = lax.axis_size("space")
    time_count = lax.axis_size("tm")
    time_slot = lax.axis_index("tm")
    space_slot = lax.axis_index("space")
    stiff_field = build_rigidity(
        rigidity, kl_coeff, space_slot * row_count, row_count * space_count, col_count
    )
    reach = 2 * (FINE + 1)
    statics = extended(jnp.stack([stiff_field, inv_mass, gust_load]), (("space", 1),), reach)
    rigid_wide = statics[0]
    mass_wide = statics[1]
    load_wide = statics[2]
    rigid_one = crop_rows(rigid_wide, reach, 1)

    def coarse_stiff(moved):
        widened = extended(moved, (("space", 0),), 2)
        return apply_padded(widened, rigid_one)

    def coarse_move(position, velocity, stiff_now, gust_value):
        return coarse_step(position, velocity, stiff_now, inv_mass, gust_load, gust_value)

    position = start_state[0, 0]
    velocity = start_state[0, 1]
    end_pos = position
    end_vel = velocity
    for sweep_index in range(ITERS):
        last_sweep = sweep_index == ITERS - 1
        both = extended(jnp.stack([position, velocity]), (("space", 1),), reach)
        rim_now = reach
        fine_stiff_now = apply_padded(both[0], crop_rows(rigid_wide, reach, rim_now - 1))
        next_rim = rim_now - 2
        first_stiff = crop_rows(fine_stiff_now, next_rim, 0)
        pos_now = crop_rows(both[0], rim_now, next_rim)
        vel_now = crop_rows(both[1], rim_now, next_rim)
        rim_now = next_rim
        for step_index in range(FINE):
            fine_gust_value = gust_history[step_index]
            mass_now = crop_rows(mass_wide, reach, rim_now)
            load_now = crop_rows(load_wide, reach, rim_now)
            half_vel = vel_now + HALF_STEP * accelerate(
                vel_now, fine_stiff_now, mass_now, load_now, fine_gust_value
            )
            pos_now = pos_now + TIME_STEP * half_vel
            fine_stiff_now = apply_padded(pos_now, crop_rows(rigid_wide, reach, rim_now - 1))
            next_rim = rim_now - 2
            pos_now = crop_rows(pos_now, rim_now, next_rim)
            half_vel = crop_rows(half_vel, rim_now, next_rim)
            mass_now = crop_rows(mass_wide, reach, next_rim)
            load_now = crop_rows(load_wide, reach, next_rim)
            vel_now = half_vel + HALF_STEP * accelerate(
                half_vel, fine_stiff_now, mass_now, load_now, fine_gust_value
            )
            rim_now = next_rim
        fine_pos, fine_vel, first_stiff = (pos_now, vel_now, first_stiff)
        coarse_pos, coarse_vel = coarse_move(position, velocity, first_stiff, gust_history[0])
        delta_pos = fine_pos - coarse_pos
        delta_vel = fine_vel - coarse_vel
        chain_pos = position
        chain_vel = velocity
        for turn_index in range(1, time_count):
            stiff_now = coarse_stiff(chain_pos)
            moved_pos, moved_vel = coarse_move(chain_pos, chain_vel, stiff_now, gust_history[0])
            outgoing = jnp.stack([moved_pos + delta_pos, moved_vel + delta_vel])
            arrived = passed_along(outgoing, "tm", 1)
            chain_pos = jnp.where(time_slot == turn_index, arrived[0], chain_pos)
            chain_vel = jnp.where(time_slot == turn_index, arrived[1], chain_vel)
        if last_sweep:
            stiff_now = coarse_stiff(chain_pos)
            moved_pos, moved_vel = coarse_move(chain_pos, chain_vel, stiff_now, gust_history[0])
            end_pos = moved_pos + delta_pos
            end_vel = moved_vel + delta_vel
        position = chain_pos
        velocity = chain_vel
    return jnp.stack([end_pos, end_vel])[None]


def solution(mesh):
    in_specs = (
        P("tm", None, "space", None),
        P("space", None),
        P("space", None),
        P("space", None),
        P(),
        P("tm"),
    )
    out_specs = P("tm", None, "space", None)
    return jax.shard_map(
        per_device, mesh=mesh, in_specs=in_specs, out_specs=out_specs, check_vma=False
    )
```

profile of v0, /device:TPU:7, one launch (start us, length us, event | category | flops | bytes accessed | tf_op | source)
XLA Modules:
  0.0 103.8 jit_solution(7189796401684182874)
XLA Ops:
  0.0 0.8 slice_bitcast_fusion.20
  0.9 3.7 %collective-permute-start.3 = (f32[2,1024]{1,0:T(2,128)S(1)}, f32[2,1024]{1,0:T(2,128)S(1)}, u32[]{:S(2)}, u32[]{:S(2)}) collective-permute-start(f32[2,1024]{1,0:T(2,128)S(1)} %get-tuple-element.43), channel_id=1, source_target_pairs={{0,1},{1,2},{2,3},{3,4},{4,5},{5,6},{6,7},{7,8},{8,9},{9,10},{10,1... | collective-permute-start | bytes 24584 | tf_op jit(solution)/shard_map/ppermute | solution.py:22
  4.6 1.9 %collective-permute-start.2 = (f32[2,1024]{1,0:T(2,128)S(1)}, f32[2,1024]{1,0:T(2,128)S(1)}, u32[]{:S(2)}, u32[]{:S(2)}) collective-permute-start(f32[2,1024]{1,0:T(2,128)S(1)} %get-tuple-element.44), channel_id=1, source_target_pairs={{1,0},{2,1},{3,2},{4,3},{5,4},{6,5},{7,6},{8,7},{9,8},{10,9},{11,1... | collective-permute-start | bytes 24584 | tf_op jit(solution)/shard_map/ppermute | solution.py:25
  6.5 1.2 %fusion.204 = f32[1024,4]{1,0:T(8,128)S(1)} fusion(f32[4,4]{1,0:T(4,128)S(1)} %copy-done, f32[1024]{0:T(1024)S(1)} %add_multiply_fusion, f32[4]{0:T(128)S(1)} %convert_multiply_fusion), kind=kOutput, calls=%fused_computation.385 | convolution fusion | flops 200704 | bytes 20560 | tf_op jit(solution)/shard_map/dot_general | solution.py:57
  7.7 1.9 %fusion.3 = f32[1,64,1024]{2,1,0:T(8,128)S(1)} fusion(f32[64,1024]{1,0:T(8,128)} %param.7, f32[1024,4]{1,0:T(8,128)S(1)} %fusion.204, f32[64]{0:T(128)S(1)} %add_multiply_fusion.1, f32[4]{0:T(128)S(1)} %convert_multiply_fusion), kind=kOutput, calls=%fused_computation.4 | convolution fusion | flops 3277056 | bytes 540944 | tf_op jit(solution)/shard_map/dot_general | solution.py:58
  9.7 4.5 %collective-permute-start = (f32[3,10,1024]{2,1,0:T(8,128)S(1)}, f32[3,10,1024]{2,1,0:T(8,128)S(1)}, u32[]{:S(2)}, u32[]{:S(2)}) collective-permute-start(f32[3,10,1024]{2,1,0:T(8,128)S(1)} %get-tuple-element.39), channel_id=1, source_target_pairs={{0,1},{1,2},{2,3},{3,4},{4,5},{5,6},{6,7},{7,8},{8,9},{9,10},{10,1... | collective-permute-start | bytes 368648 | tf_op jit(solution)/shard_map/ppermute | solution.py:22
  14.2 1.9 %collective-permute-start.1 = (f32[3,10,1024]{2,1,0:T(8,128)S(1)}, f32[3,10,1024]{2,1,0:T(8,128)S(1)}, u32[]{:S(2)}, u32[]{:S(2)}) collective-permute-start(f32[3,10,1024]{2,1,0:T(8,128)S(1)} %get-tuple-element.40), channel_id=1, source_target_pairs={{1,0},{2,1},{3,2},{4,3},{5,4},{6,5},{7,6},{8,7},{9,8},{10,9},{11,1... | collective-permute-start | bytes 368648 | tf_op jit(solution)/shard_map/ppermute | solution.py:25
  16.3 4.5 %collective-permute-start.4 = (f32[2,10,1024]{2,1,0:T(8,128)S(1)}, f32[2,10,1024]{2,1,0:T(8,128)S(1)}, u32[]{:S(2)}, u32[]{:S(2)}) collective-permute-start(f32[2,10,1024]{2,1,0:T(8,128)S(1)} %get-tuple-element.48), channel_id=1, source_target_pairs={{0,1},{1,2},{2,3},{3,4},{4,5},{5,6},{6,7},{7,8},{8,9},{9,10},{10,1... | collective-permute-start | bytes 245768 | tf_op jit(solution)/shard_map/ppermute | solution.py:22
  20.8 0.6 fusion.228
  21.4 1.9 %collective-permute-start.5 = (f32[2,10,1024]{2,1,0:T(8,128)S(1)}, f32[2,10,1024]{2,1,0:T(8,128)S(1)}, u32[]{:S(2)}, u32[]{:S(2)}) collective-permute-start(f32[2,10,1024]{2,1,0:T(8,128)S(1)} %get-tuple-element.49), channel_id=1, source_target_pairs={{1,0},{2,1},{3,2},{4,3},{5,4},{6,5},{7,6},{8,7},{9,8},{10,9},{11,1... | collective-permute-start | bytes 245768 | tf_op jit(solution)/shard_map/ppermute | solution.py:25
  23.4 5.2 %collective-permute-done.5 = f32[2,10,1024]{2,1,0:T(8,128)S(1)} collective-permute-done((f32[2,10,1024]{2,1,0:T(8,128)S(1)}, f32[2,10,1024]{2,1,0:T(8,128)S(1)}, u32[]{:S(2)}, u32[]{:S(2)}) %collective-permute-start.5) | collective-permute-done | bytes 81952 | tf_op jit(solution)/shard_map/ppermute | solution.py:25
  28.9 0.3 fusion.7
  29.2 1.0 fusion.50
  30.2 0.2 fusion.19
  30.4 1.7 %slice_add_fusion.10 = (f32[76,1024]{1,0:T(8,128)S(1)}, f32[76,1024]{1,0:T(8,128)S(1)}) fusion(f32[80,1024]{1,0:T(8,128)S(1)} %get-tuple-element.30, f32[]{:T(128)} %bitcast.22, f32[78,1024]{1,0:T(8,128)S(1)} %fusion.19, f32[]{:T(128)} %bitcast.2, f32[3,84,1024]{2,1,0:T(8,128)S(1)} %pad_maximum_fusion, f32[80,1024]{1,0:T(8,128)S(1)} %get-tuple-element.31), kind=kLoop, calls=%fused_computation.135 | loop fusion | flops 1712128 | bytes 3244040 | tf_op jit(solution)/shard_map/add | solution.py:129
  32.1 0.2 fusion.27
  32.4 1.7 %slice_add_fusion.23 = (f32[72,1024]{1,0:T(8,128)S(1)}, f32[72,1024]{1,0:T(8,128)S(1)}) fusion(f32[76,1024]{1,0:T(8,128)S(1)} %get-tuple-element.28, f32[]{:T(128)} %bitcast.27, f32[74,1024]{1,0:T(8,128)S(1)} %fusion.27, f32[]{:T(128)} %bitcast.22, f32[3,84,1024]{2,1,0:T(8,128)S(1)} %pad_maximum_fusion, f32[76,1024]{1,0:T(8,128)S(1)} %get-tuple-element.29), kind=kLoop, calls=%fused_computation.236 | loop fusion | flops 1622016 | bytes 2981896 | tf_op jit(solution)/shard_map/add | solution.py:129
  34.1 0.2 fusion.74
  34.3 1.7 %slice_add_fusion.21 = (f32[68,1024]{1,0:T(8,128)S(1)}, f32[68,1024]{1,0:T(8,128)S(1)}) fusion(f32[72,1024]{1,0:T(8,128)S(1)} %get-tuple-element.26, f32[]{:T(128)} %bitcast.32, f32[70,1024]{1,0:T(8,128)S(1)} %fusion.74, f32[]{:T(128)} %bitcast.27, f32[3,84,1024]{2,1,0:T(8,128)S(1)} %pad_maximum_fusion, f32[72,1024]{1,0:T(8,128)S(1)} %get-tuple-element.27), kind=kLoop, calls=%fused_computation.232 | loop fusion | flops 1531904 | bytes 2916360 | tf_op jit(solution)/shard_map/add | solution.py:129
  36.0 0.4 fusion.82
  36.4 0.9 fusion.203
  37.3 1.6 %fusion.163 = f32[1,64,1024]{2,1,0:T(8,128)S(1)} fusion(f32[64,1024]{1,0:T(8,128)S(1)} %get-tuple-element.23, f32[64,1024]{1,0:T(8,128)S(1)} %copy-done.2, f32[66,1024]{1,0:T(8,128)S(1)} %get-tuple-element.35, f32[68,1024]{1,0:T(8,128)S(1)} %get-tuple-element.25, f32[64,1024]{1,0:T(8,128)S(1)} %copy-done.1, f32[]{:T(128)} %bitcast.32, ...), kind=kLoop, calls=%fused_computation.309 | loop fusion | flops 1441792 | bytes 2916360 | tf_op jit(solution)/shard_map/stack | solution.py:149
  38.9 1.3 %collective-permute-start.6 = (f32[2,64,1024]{2,1,0:T(8,128)S(1)}, f32[2,64,1024]{2,1,0:T(8,128)S(1)}, u32[]{:S(2)}, u32[]{:S(2)}) collective-permute-start(f32[2,64,1024]{2,1,0:T(8,128)S(1)} %pad_maximum_fusion.3), channel_id=1, source_target_pairs={{0,16},{1,17},{2,18},{3,19},{4,20},{5,21},{6,22},{7,23},{8,24},{9,... | collective-permute-start | bytes 1572872 | tf_op jit(solution)/shard_map/ppermute | solution.py:33
  40.2 10.8 %collective-permute-done.6 = f32[2,64,1024]{2,1,0:T(8,128)S(1)} collective-permute-done((f32[2,64,1024]{2,1,0:T(8,128)S(1)}, f32[2,64,1024]{2,1,0:T(8,128)S(1)}, u32[]{:S(2)}, u32[]{:S(2)}) %collective-permute-start.6) | collective-permute-done | bytes 524320 | tf_op jit(solution)/shard_map/ppermute | solution.py:33
  51.0 4.5 %collective-permute-start.8 = (f32[2,1024]{1,0:T(2,128)S(1)}, f32[2,1024]{1,0:T(2,128)S(1)}, u32[]{:S(2)}, u32[]{:S(2)}) collective-permute-start(f32[2,1024]{1,0:T(2,128)S(1)} %get-tuple-element.52), channel_id=1, source_target_pairs={{0,1},{1,2},{2,3},{3,4},{4,5},{5,6},{6,7},{7,8},{8,9},{9,10},{10,1... | collective-permute-start | bytes 24584 | tf_op jit(solution)/shard_map/ppermute | solution.py:22
  55.5 1.9 %collective-permute-start.7 = (f32[2,1024]{1,0:T(2,128)S(1)}, f32[2,1024]{1,0:T(2,128)S(1)}, u32[]{:S(2)}, u32[]{:S(2)}) collective-permute-start(f32[2,1024]{1,0:T(2,128)S(1)} %get-tuple-element.53), channel_id=1, source_target_pairs={{1,0},{2,1},{3,2},{4,3},{5,4},{6,5},{7,6},{8,7},{9,8},{10,9},{11,1... | collective-permute-start | bytes 24584 | tf_op jit(solution)/shard_map/ppermute | solution.py:25
  57.5 4.5 %collective-permute-start.9 = (f32[2,10,1024]{2,1,0:T(8,128)S(1)}, f32[2,10,1024]{2,1,0:T(8,128)S(1)}, u32[]{:S(2)}, u32[]{:S(2)}) collective-permute-start(f32[2,10,1024]{2,1,0:T(8,128)S(1)} %get-tuple-element.41), channel_id=1, source_target_pairs={{0,1},{1,2},{2,3},{3,4},{4,5},{5,6},{6,7},{7,8},{8,9},{9,10},{10,1... | collective-permute-start | bytes 245768 | tf_op jit(solution)/shard_map/ppermute | solution.py:22
  62.1 1.9 %collective-permute-start.10 = (f32[2,10,1024]{2,1,0:T(8,128)S(1)}, f32[2,10,1024]{2,1,0:T(8,128)S(1)}, u32[]{:S(2)}, u32[]{:S(2)}) collective-permute-start(f32[2,10,1024]{2,1,0:T(8,128)S(1)} %get-tuple-element.42), channel_id=1, source_target_pairs={{1,0},{2,1},{3,2},{4,3},{5,4},{6,5},{7,6},{8,7},{9,8},{10,9},{11,1... | collective-permute-start | bytes 245768 | tf_op jit(solution)/shard_map/ppermute | solution.py:25
  64.1 5.2 %collective-permute-done.10 = f32[2,10,1024]{2,1,0:T(8,128)S(1)} collective-permute-done((f32[2,10,1024]{2,1,0:T(8,128)S(1)}, f32[2,10,1024]{2,1,0:T(8,128)S(1)}, u32[]{:S(2)}, u32[]{:S(2)}) %collective-permute-start.10) | collective-permute-done | bytes 81952 | tf_op jit(solution)/shard_map/ppermute | solution.py:25
  69.4 0.3 fusion.11
  69.7 1.0 fusion.48
  70.7 0.2 fusion.31
  70.9 1.7 %slice_add_fusion.5 = (f32[76,1024]{1,0:T(8,128)S(1)}, f32[76,1024]{1,0:T(8,128)S(1)}) fusion(f32[80,1024]{1,0:T(8,128)S(1)} %get-tuple-element.19, f32[]{:T(128)} %bitcast.22, f32[78,1024]{1,0:T(8,128)S(1)} %fusion.31, f32[]{:T(128)} %bitcast.2, f32[3,84,1024]{2,1,0:T(8,128)S(1)} %pad_maximum_fusion, f32[80,1024]{1,0:T(8,128)S(1)} %get-tuple-element.20), kind=kLoop, calls=%fused_computation.120 | loop fusion | flops 1712128 | bytes 3244040 | tf_op jit(solution)/shard_map/add | solution.py:129
  72.6 0.2 fusion.39
  72.9 1.7 %slice_add_fusion.17 = (f32[72,1024]{1,0:T(8,128)S(1)}, f32[72,1024]{1,0:T(8,128)S(1)}) fusion(f32[76,1024]{1,0:T(8,128)S(1)} %get-tuple-element.17, f32[]{:T(128)} %bitcast.27, f32[74,1024]{1,0:T(8,128)S(1)} %fusion.39, f32[]{:T(128)} %bitcast.22, f32[3,84,1024]{2,1,0:T(8,128)S(1)} %pad_maximum_fusion, f32[76,1024]{1,0:T(8,128)S(1)} %get-tuple-element.18), kind=kLoop, calls=%fused_computation.222 | loop fusion | flops 1622016 | bytes 2981896 | tf_op jit(solution)/shard_map/add | solution.py:129
  74.6 0.2 fusion.90
  74.8 1.7 %slice_add_fusion.15 = (f32[68,1024]{1,0:T(8,128)S(1)}, f32[68,1024]{1,0:T(8,128)S(1)}) fusion(f32[72,1024]{1,0:T(8,128)S(1)} %get-tuple-element.15, f32[]{:T(128)} %bitcast.32, f32[70,1024]{1,0:T(8,128)S(1)} %fusion.90, f32[]{:T(128)} %bitcast.27, f32[3,84,1024]{2,1,0:T(8,128)S(1)} %pad_maximum_fusion, f32[72,1024]{1,0:T(8,128)S(1)} %get-tuple-element.16), kind=kLoop, calls=%fused_computation.219 | loop fusion | flops 1531904 | bytes 2916360 | tf_op jit(solution)/shard_map/add | solution.py:129
  76.5 0.4 fusion.98
  76.9 1.0 add_bitcast_fusion.3
  77.8 1.0 add_bitcast_fusion.2
  78.8 1.3 %collective-permute-start.11 = (f32[2,64,1024]{2,1,0:T(8,128)S(1)}, f32[2,64,1024]{2,1,0:T(8,128)S(1)}, u32[]{:S(2)}, u32[]{:S(2)}) collective-permute-start(f32[2,64,1024]{2,1,0:T(8,128)S(1)} %pad_maximum_fusion.4), channel_id=1, source_target_pairs={{0,16},{1,17},{2,18},{3,19},{4,20},{5,21},{6,22},{7,23},{8,24},{9,... | collective-permute-start | bytes 1572872 | tf_op jit(solution)/shard_map/ppermute | solution.py:33
  80.1 10.8 %collective-permute-done.11 = f32[2,64,1024]{2,1,0:T(8,128)S(1)} collective-permute-done((f32[2,64,1024]{2,1,0:T(8,128)S(1)}, f32[2,64,1024]{2,1,0:T(8,128)S(1)}, u32[]{:S(2)}, u32[]{:S(2)}) %collective-permute-start.11) | collective-permute-done | bytes 524320 | tf_op jit(solution)/shard_map/ppermute | solution.py:33
  90.9 4.9 %collective-permute-start.13 = (f32[2,1024]{1,0:T(2,128)S(1)}, f32[2,1024]{1,0:T(2,128)S(1)}, u32[]{:S(2)}, u32[]{:S(2)}) collective-permute-start(f32[2,1024]{1,0:T(2,128)S(1)} %get-tuple-element.50), channel_id=1, source_target_pairs={{0,1},{1,2},{2,3},{3,4},{4,5},{5,6},{6,7},{7,8},{8,9},{9,10},{10,1... | collective-permute-start | bytes 24584 | tf_op jit(solution)/shard_map/ppermute | solution.py:22
  95.8 1.9 %collective-permute-start.12 = (f32[2,1024]{1,0:T(2,128)S(1)}, f32[2,1024]{1,0:T(2,128)S(1)}, u32[]{:S(2)}, u32[]{:S(2)}) collective-permute-start(f32[2,1024]{1,0:T(2,128)S(1)} %get-tuple-element.51), channel_id=1, source_target_pairs={{1,0},{2,1},{3,2},{4,3},{5,4},{6,5},{7,6},{8,7},{9,8},{10,9},{11,1... | collective-permute-start | bytes 24584 | tf_op jit(solution)/shard_map/ppermute | solution.py:25
  97.8 3.9 %collective-permute-done.12 = f32[2,1024]{1,0:T(2,128)S(1)} collective-permute-done((f32[2,1024]{1,0:T(2,128)S(1)}, f32[2,1024]{1,0:T(2,128)S(1)}, u32[]{:S(2)}, u32[]{:S(2)}) %collective-permute-start.12) | collective-permute-done | bytes 8224 | tf_op jit(solution)/shard_map/ppermute | solution.py:25
  101.7 0.2 fusion.102
  102.0 0.9 add_bitcast_fusion.1
  102.9 0.8 maximum_bitcast_fusion
  (42 shorter events, 0.9 us)
Async XLA Ops:
  0.0 6.5 %copy-start = (f32[4,4]{1,0:T(4,128)S(1)}, f32[4,4]{1,0:T(4,128)}, u32[]{:S(2)}) copy-start(f32[4,4]{1,0:T(4,128)} %param.10) | copy-start | bytes 196
  0.0 9.6 %copy-start.2 = (f32[64,1024]{1,0:T(8,128)S(1)}, f32[64,1024]{1,0:T(8,128)}, u32[]{:S(2)}) copy-start(f32[64,1024]{1,0:T(8,128)} %param.8) | copy-start | bytes 786436
  0.0 9.6 %copy-start.1 = (f32[64,1024]{1,0:T(8,128)S(1)}, f32[64,1024]{1,0:T(8,128)}, u32[]{:S(2)}) copy-start(f32[64,1024]{1,0:T(8,128)} %param.9) | copy-start | bytes 786436
  0.9 20.6 %collective-permute-start.3 = (f32[2,1024]{1,0:T(2,128)S(1)}, f32[2,1024]{1,0:T(2,128)S(1)}, u32[]{:S(2)}, u32[]{:S(2)}) collective-permute-start(f32[2,1024]{1,0:T(2,128)S(1)} %get-tuple-element.43), channel_id=1, source_target_pairs={{0,1},{1,2},{2,3},{3,4},{4,5},{5,6},{6,7},{7,8},{8,9},{9,10},{10,1... | collective-permute-start | bytes 24584 | tf_op jit(solution)/shard_map/ppermute | solution.py:22
  4.6 18.8 %collective-permute-start.2 = (f32[2,1024]{1,0:T(2,128)S(1)}, f32[2,1024]{1,0:T(2,128)S(1)}, u32[]{:S(2)}, u32[]{:S(2)}) collective-permute-start(f32[2,1024]{1,0:T(2,128)S(1)} %get-tuple-element.44), channel_id=1, source_target_pairs={{1,0},{2,1},{3,2},{4,3},{5,4},{6,5},{7,6},{8,7},{9,8},{10,9},{11,1... | collective-permute-start | bytes 24584 | tf_op jit(solution)/shard_map/ppermute | solution.py:25
  7.7 8.4 %copy-start.3 = (f32[1,2,64,1024]{3,2,1,0:T(8,128)S(1)}, f32[1,2,64,1024]{3,2,1,0:T(8,128)}, u32[]{:S(2)}) copy-start(f32[1,2,64,1024]{3,2,1,0:T(8,128)} %param.6) | copy-start | bytes 1572868
  9.6 11.2 %copy-start.4 = (f32[4]{0:T(128)S(1)}, f32[4]{0:T(128)}, u32[]{:S(2)}) copy-start(f32[4]{0:T(128)} %param.11) | copy-start | bytes 52
  9.7 19.1 %collective-permute-start = (f32[3,10,1024]{2,1,0:T(8,128)S(1)}, f32[3,10,1024]{2,1,0:T(8,128)S(1)}, u32[]{:S(2)}, u32[]{:S(2)}) collective-permute-start(f32[3,10,1024]{2,1,0:T(8,128)S(1)} %get-tuple-element.39), channel_id=1, source_target_pairs={{0,1},{1,2},{2,3},{3,4},{4,5},{5,6},{6,7},{7,8},{8,9},{9,10},{10,1... | collective-permute-start | bytes 368648 | tf_op jit(solution)/shard_map/ppermute | solution.py:22
  14.2 14.5 %collective-permute-start.1 = (f32[3,10,1024]{2,1,0:T(8,128)S(1)}, f32[3,10,1024]{2,1,0:T(8,128)S(1)}, u32[]{:S(2)}, u32[]{:S(2)}) collective-permute-start(f32[3,10,1024]{2,1,0:T(8,128)S(1)} %get-tuple-element.40), channel_id=1, source_target_pairs={{1,0},{2,1},{3,2},{4,3},{5,4},{6,5},{7,6},{8,7},{9,8},{10,9},{11,1... | collective-permute-start | bytes 368648 | tf_op jit(solution)/shard_map/ppermute | solution.py:25
  16.3 7.2 %collective-permute-start.4 = (f32[2,10,1024]{2,1,0:T(8,128)S(1)}, f32[2,10,1024]{2,1,0:T(8,128)S(1)}, u32[]{:S(2)}, u32[]{:S(2)}) collective-permute-start(f32[2,10,1024]{2,1,0:T(8,128)S(1)} %get-tuple-element.48), channel_id=1, source_target_pairs={{0,1},{1,2},{2,3},{3,4},{4,5},{5,6},{6,7},{7,8},{8,9},{9,10},{10,1... | collective-permute-start | bytes 245768 | tf_op jit(solution)/shard_map/ppermute | solution.py:22
  21.4 7.2 %collective-permute-start.5 = (f32[2,10,1024]{2,1,0:T(8,128)S(1)}, f32[2,10,1024]{2,1,0:T(8,128)S(1)}, u32[]{:S(2)}, u32[]{:S(2)}) collective-permute-start(f32[2,10,1024]{2,1,0:T(8,128)S(1)} %get-tuple-element.49), channel_id=1, source_target_pairs={{1,0},{2,1},{3,2},{4,3},{5,4},{6,5},{7,6},{8,7},{9,8},{10,9},{11,1... | collective-permute-start | bytes 245768 | tf_op jit(solution)/shard_map/ppermute | solution.py:25
  38.9 12.1 %collective-permute-start.6 = (f32[2,64,1024]{2,1,0:T(8,128)S(1)}, f32[2,64,1024]{2,1,0:T(8,128)S(1)}, u32[]{:S(2)}, u32[]{:S(2)}) collective-permute-start(f32[2,64,1024]{2,1,0:T(8,128)S(1)} %pad_maximum_fusion.3), channel_id=1, source_target_pairs={{0,16},{1,17},{2,18},{3,19},{4,20},{5,21},{6,22},{7,23},{8,24},{9,... | collective-permute-start | bytes 1572872 | tf_op jit(solution)/shard_map/ppermute | solution.py:33
  51.0 13.0 %collective-permute-start.8 = (f32[2,1024]{1,0:T(2,128)S(1)}, f32[2,1024]{1,0:T(2,128)S(1)}, u32[]{:S(2)}, u32[]{:S(2)}) collective-permute-start(f32[2,1024]{1,0:T(2,128)S(1)} %get-tuple-element.52), channel_id=1, source_target_pairs={{0,1},{1,2},{2,3},{3,4},{4,5},{5,6},{6,7},{7,8},{8,9},{9,10},{10,1... | collective-permute-start | bytes 24584 | tf_op jit(solution)/shard_map/ppermute | solution.py:22
  55.5 8.5 %collective-permute-start.7 = (f32[2,1024]{1,0:T(2,128)S(1)}, f32[2,1024]{1,0:T(2,128)S(1)}, u32[]{:S(2)}, u32[]{:S(2)}) collective-permute-start(f32[2,1024]{1,0:T(2,128)S(1)} %get-tuple-element.53), channel_id=1, source_target_pairs={{1,0},{2,1},{3,2},{4,3},{5,4},{6,5},{7,6},{8,7},{9,8},{10,9},{11,1... | collective-permute-start | bytes 24584 | tf_op jit(solution)/shard_map/ppermute | solution.py:25
  57.5 6.5 %collective-permute-start.9 = (f32[2,10,1024]{2,1,0:T(8,128)S(1)}, f32[2,10,1024]{2,1,0:T(8,128)S(1)}, u32[]{:S(2)}, u32[]{:S(2)}) collective-permute-start(f32[2,10,1024]{2,1,0:T(8,128)S(1)} %get-tuple-element.41), channel_id=1, source_target_pairs={{0,1},{1,2},{2,3},{3,4},{4,5},{5,6},{6,7},{7,8},{8,9},{9,10},{10,1... | collective-permute-start | bytes 245768 | tf_op jit(solution)/shard_map/ppermute | solution.py:22
  62.1 7.2 %collective-permute-start.10 = (f32[2,10,1024]{2,1,0:T(8,128)S(1)}, f32[2,10,1024]{2,1,0:T(8,128)S(1)}, u32[]{:S(2)}, u32[]{:S(2)}) collective-permute-start(f32[2,10,1024]{2,1,0:T(8,128)S(1)} %get-tuple-element.42), channel_id=1, source_target_pairs={{1,0},{2,1},{3,2},{4,3},{5,4},{6,5},{7,6},{8,7},{9,8},{10,9},{11,1... | collective-permute-start | bytes 245768 | tf_op jit(solution)/shard_map/ppermute | solution.py:25
  78.8 12.1 %collective-permute-start.11 = (f32[2,64,1024]{2,1,0:T(8,128)S(1)}, f32[2,64,1024]{2,1,0:T(8,128)S(1)}, u32[]{:S(2)}, u32[]{:S(2)}) collective-permute-start(f32[2,64,1024]{2,1,0:T(8,128)S(1)} %pad_maximum_fusion.4), channel_id=1, source_target_pairs={{0,16},{1,17},{2,18},{3,19},{4,20},{5,21},{6,22},{7,23},{8,24},{9,... | collective-permute-start | bytes 1572872 | tf_op jit(solution)/shard_map/ppermute | solution.py:33
  90.9 6.8 %collective-permute-start.13 = (f32[2,1024]{1,0:T(2,128)S(1)}, f32[2,1024]{1,0:T(2,128)S(1)}, u32[]{:S(2)}, u32[]{:S(2)}) collective-permute-start(f32[2,1024]{1,0:T(2,128)S(1)} %get-tuple-element.50), channel_id=1, source_target_pairs={{0,1},{1,2},{2,3},{3,4},{4,5},{5,6},{6,7},{7,8},{8,9},{9,10},{10,1... | collective-permute-start | bytes 24584 | tf_op jit(solution)/shard_map/ppermute | solution.py:22
  95.8 5.9 %collective-permute-start.12 = (f32[2,1024]{1,0:T(2,128)S(1)}, f32[2,1024]{1,0:T(2,128)S(1)}, u32[]{:S(2)}, u32[]{:S(2)}) collective-permute-start(f32[2,1024]{1,0:T(2,128)S(1)} %get-tuple-element.51), channel_id=1, source_target_pairs={{1,0},{2,1},{3,2},{4,3},{5,4},{6,5},{7,6},{8,7},{9,8},{10,9},{11,1... | collective-permute-start | bytes 24584 | tf_op jit(solution)/shard_map/ppermute | solution.py:25
where the time goes:
time: 104 us
  starting transfers between devices  40.8 us (39%)
  waiting for transfers between devices  35.9 us (35%)
  other arithmetic  22 us (21%)
  matrix products  3.02 us (3%)
  local copies, waits for them, and re-layouts  1.62 us (2%)
    ppermute x6, starting transfers between devices, extended(): lax.ppermute(lax.slice_in_dim(block, block.shape[dim] - width, None, axis...  26.7 us
    ppermute x2, waiting for transfers between devices, passed_along(): return lax.ppermute(block, axis, route)  21.5 us
    ppermute x6, waiting for transfers between devices, extended(): lax.ppermute(lax.slice_in_dim(block, 0, width, axis=dim), axis, backward)  14.3 us
    add x8, other arithmetic, per_device(): pos_now = pos_now + TIME_STEP * half_vel  12.2 us
    ppermute x6, starting transfers between devices, extended(): lax.ppermute(lax.slice_in_dim(block, 0, width, axis=dim), axis, backward)  11.5 us
    another operation x6, other arithmetic, per_device(): outgoing = jnp.stack([moved_pos + delta_pos, moved_vel + delta_vel])  4.47 us
    mul x11, other arithmetic, apply_padded(): weighted = rigid_rim * laplace(jnp.pad(widened, ((0, 0), (1, 1))))  2.92 us
    ppermute x2, starting transfers between devices, passed_along(): return lax.ppermute(block, axis, route)  2.58 us
  transfers between devices with their start and end apart: 14, of which 5 were waited for; matrix products, arithmetic and copies ran while one was open for 4% of the time, Pallas kernels for 0%

commit v1 on v0

--- a/solution.py
+++ b/solution.py
@@ -1,6 +1,10 @@
+import functools
+
 import jax
 import jax.numpy as jnp
 from jax import lax
+from jax.experimental import pallas as pl
+from jax.experimental.pallas import tpu as pltpu
 from jax.sharding import PartitionSpec as P
 
 FINE = 4
@@ -160,6 +164,311 @@
     return jnp.stack([end_pos, end_vel])[None]
 
 
+LANES = 128
+SUBLANES = 8
+COARSE_SPAN = FINE * TIME_STEP
+DECAY = 1.0 - HALF_STEP * DAMPING
+COARSE_DECAY = 1.0 - COARSE_SPAN * DAMPING
+KICK = TIME_STEP * HALF_STEP
+UNROLL = 8
+
+
+def tile_view(block):
+    width = block.shape[-1] // LANES
+    tiles = block.reshape(-1, SUBLANES, width, LANES).transpose(0, 2, 1, 3)
+    return tiles.reshape(-1, LANES)
+
+
+def from_tile_view(view, shape):
+    width = shape[-1] // LANES
+    tiles = view.reshape(-1, width, SUBLANES, LANES).transpose(0, 2, 1, 3)
+    return tiles.reshape(shape)
+
+
+def row_at(view_ref, group, row):
+    start = pl.multiple_of(group * SUBLANES * SUBLANES, SUBLANES * SUBLANES)
+    return view_ref[pl.ds(start + row, SUBLANES, stride=SUBLANES), :]
+
+
+def pack_kernel(gust_ref, view_ref, edge_ref, mid_ref, *, rows, far, near):
+    sub = lax.broadcasted_iota(jnp.int32, (SUBLANES, LANES), 0)
+    gusts = jnp.zeros((SUBLANES, LANES), jnp.float32)
+    for step_index in range(FINE):
+        gusts = jnp.where(sub == step_index, gust_ref[step_index], gusts)
+    side = far + near
+    edge_ref[2 * side] = gusts
+    for part, width, at in ((0, far, 0), (1, near, far)):
+        for row in range(rows):
+            group = (part * rows + row) // SUBLANES
+            value = row_at(view_ref, group, row % SUBLANES)
+            if row < width:
+                edge_ref[at + row] = value
+            elif row >= rows - width:
+                edge_ref[side + at + row - (rows - width)] = value
+            else:
+                mid_ref[part * (rows - 2 * far) + row - width] = value
+
+
+def field_kernel(
+    kl_ref, across_ref, along_ref, rigid_ref, mass_ref, load_ref, stiff_ref, pull_ref, push_ref
+):
+    rows = stiff_ref.shape[0]
+    mixed = []
+    for order in range(KL):
+        total = kl_ref[order, 0] * along_ref[0]
+        for other in range(1, KL):
+            total = total + kl_ref[order, other] * along_ref[other]
+        mixed.append(total)
+
+    def group_rows(group, carry):
+        for row in range(SUBLANES):
+            at = group * SUBLANES + row
+            field = across_ref[0, at] * mixed[0]
+            for order in range(1, KL):
+                field = field + across_ref[order, at] * mixed[order]
+            mass = row_at(mass_ref, group, row)
+            stiff_ref[at] = row_at(rigid_ref, group, row) * jnp.exp(0.5 * jnp.tanh(field))
+            pull_ref[at] = (KICK * (1.0 + DECAY) * STIFF_SCALE) * mass
+            push_ref[at] = KICK * (mass * row_at(load_ref, group, row))
+        return carry
+
+    lax.fori_loop(0, rows // SUBLANES, group_rows, 0)
+
+
+def chain_kernel(
+    slot_ref, pos_in, vel_in, stiff_ref, pull_ref, push_ref, gust_ref, out_ref,
+    pos, vel, coarse_pos, coarse_vel, *, rows, far
+):
+    near = far - 2
+    lane = lax.broadcasted_iota(jnp.int32, (SUBLANES, LANES), 1)
+    sub = lax.broadcasted_iota(jnp.int32, (SUBLANES, LANES), 0)
+    last_lane = lane == LANES - 1
+    first_lane = lane == 0
+    low_corner = last_lane & (sub == 0)
+    high_corner = first_lane & (sub == SUBLANES - 1)
+    half_pull = 1.0 / (1.0 + DECAY)
+    slot = slot_ref[0]
+
+    def gust(stage, step_index):
+        return jnp.broadcast_to(gust_ref[stage, step_index:step_index + 1, :], (SUBLANES, LANES))
+
+    def beside(row):
+        below = jnp.where(last_lane, pltpu.roll(row, 1, 0), row)
+        above = jnp.where(first_lane, pltpu.roll(row, SUBLANES - 1, 0), row)
+        below = jnp.where(low_corner, 0.0, below)
+        above = jnp.where(high_corner, 0.0, above)
+        return pltpu.roll(below, 1, 1) + pltpu.roll(above, LANES - 1, 1)
+
+    def sweep(source, margin, update):
+        count = -(-(rows + 2 * margin) // UNROLL) * UNROLL
+        first = min(-margin, rows + near - count)
+
+        def weigh(row, before, here, after):
+            return stiff_ref[row + far - 1] * (before + after + beside(here) - 4.0 * here)
+
+        start = [source[first - 2 + far + i] for i in range(4)]
+        carry = (
+            weigh(first - 1, start[0], start[1], start[2]),
+            weigh(first, start[1], start[2], start[3]),
+            start[2],
+            start[3],
+        )
+
+        def chunk(index, carry):
+            base = first + index * UNROLL
+            w_before, w_here, p_here, p_after = carry
+            for j in range(UNROLL):
+                p_next = source[base + j + 2 + far]
+                w_after = weigh(base + j + 1, p_here, p_after, p_next)
+                bent = w_before + w_after + beside(w_here) - 4.0 * w_here
+                update(index, j, base + j, p_here, bent)
+                w_before, w_here, p_here, p_after = w_here, w_after, p_after, p_next
+            return w_before, w_here, p_here, p_after
+
+        lax.fori_loop(0, count // UNROLL, chunk, carry)
+
+    def start_slice(row, position, velocity, bent, gust_value):
+        force = gust_value * push_ref[row + near] - half_pull * (pull_ref[row + near] * bent)
+        shift = (TIME_STEP * DECAY) * velocity + force
+        new_vel = COARSE_DECAY * velocity + (COARSE_SPAN / KICK) * force
+        coarse_vel[row + near] = new_vel
+        coarse_pos[row + near] = position + COARSE_SPAN * new_vel
+        vel[row + near] = shift
+        pos[row + far] = position + shift
+
+    def advance(gust_value, joins):
+        def update(index, j, row, position, bent):
+            shift = (
+                (DECAY * DECAY) * vel[row + near]
+                + gust_value * push_ref[row + near]
+                - pull_ref[row + near] * bent
+            )
+            vel[row + near] = shift
+            moved = position + shift
+            if joins:
+                coarse = coarse_pos[row + near]
+                moved = coarse + (moved - coarse)
+            pos[row + far] = moved
+
+        return update
+
+    def end_velocity(row, bent, gust_value):
+        force = gust_value * push_ref[row + near] - half_pull * (pull_ref[row + near] * bent)
+        fine_vel = (1.0 / TIME_STEP) * (DECAY * vel[row + near] + force)
+        coarse = coarse_vel[row + near]
+        return coarse + (fine_vel - coarse)
+
+    def finish(gust_value):
+        def update(index, j, row, position, bent):
+            group = index * (UNROLL // SUBLANES) + j // SUBLANES
+            start = pl.multiple_of(group * SUBLANES * SUBLANES, SUBLANES * SUBLANES)
+            at = start + j % SUBLANES
+            out_ref[pl.ds(at, SUBLANES, stride=SUBLANES), :] = position
+            out_ref[pl.ds(at + rows * SUBLANES, SUBLANES, stride=SUBLANES), :] = end_velocity(
+                row, bent, gust_value
+            )
+
+        return update
+
+    def fine_steps(stage, margin):
+        for step_index in range(1, FINE):
+            gust_value = DECAY * gust(stage, step_index - 1) + gust(stage, step_index)
+            margin -= 2
+            sweep(pos, margin, advance(gust_value, step_index == FINE - 1))
+        return margin
+
+    blank = jnp.zeros((SUBLANES, LANES), jnp.float32)
+    for row in (-far, -far + 1, rows + far - 2, rows + far - 1):
+        pos[row + far] = blank
+    first_gust = gust(0, 0)
+    sweep(
+        pos_in,
+        near,
+        lambda index, j, row, position, bent: start_slice(
+            row, position, vel_in[row + near], bent, first_gust
+        ),
+    )
+    margin = fine_steps(0, near) - 2
+
+    @pl.when(slot == 0)
+    def _():
+        sweep(pos, 0, finish(gust(0, FINE - 1)))
+
+    @pl.when(slot != 0)
+    def _():
+        last_gust = gust(0, FINE - 1)
+        next_gust = gust(1, 0)
+
+        def link(index, j, row, position, bent):
+            velocity = end_velocity(row, bent, last_gust)
+            start_slice(row, position, velocity, bent, next_gust)
+
+        sweep(pos, margin, link)
+        fine_steps(1, margin)
+        sweep(pos, 0, finish(gust(1, FINE - 1)))
+
+
+def swap_pairs(count, first):
+    pairs = [(i, i + 1) for i in range(first, count - 1, 2)]
+    return pairs + [(target, source) for source, target in pairs]
+
+
+def exchanged(low_rows, high_rows, odd):
+    count = lax.axis_size("space")
+    inner = lax.ppermute(jnp.where(odd, low_rows, high_rows), "space", swap_pairs(count, 0))
+    outer = lax.ppermute(jnp.where(odd, high_rows, low_rows), "space", swap_pairs(count, 1))
+    return jnp.where(odd, inner, outer), jnp.where(odd, outer, inner)
+
+
+def in_vmem(count):
+    return [pl.BlockSpec(memory_space=pltpu.VMEM)] * count
+
+
+def in_smem(count):
+    return [pl.BlockSpec(memory_space=pltpu.SMEM)] * count
+
+
+def plane(count):
+    return jax.ShapeDtypeStruct((count, SUBLANES, LANES), jnp.float32)
+
+
+def two_slice_device(start_state, rigidity, inv_mass, gust_load, kl_coeff, gust_history):
+    rows, cols = rigidity.shape
+    far = 2 * (2 * FINE + 1)
+    near = far - 2
+    side = far + near
+    time_slot = lax.axis_index("tm")
+    space_slot = lax.axis_index("space")
+    odd = space_slot % 2 == 1
+    small = pltpu.CompilerParams(vmem_limit_bytes=16 * 2**20)
+
+    edge_own, mid_own = pl.pallas_call(
+        functools.partial(pack_kernel, rows=rows, far=far, near=near),
+        out_shape=(plane(2 * side + 1), plane(2 * rows - 2 * side)),
+        in_specs=in_smem(1) + in_vmem(1),
+        out_specs=tuple(in_vmem(2)),
+        compiler_params=small,
+        name="pack",
+    )(gust_history, tile_view(start_state))
+    edge_in = passed_along(edge_own, "tm", 1)
+    mid_in = passed_along(mid_own, "tm", 1)
+
+    across = mode_table(space_slot * rows + jnp.arange(rows), rows * lax.axis_size("space"))
+    along = mode_table(jnp.arange(cols), cols).reshape(KL, SUBLANES, LANES)
+    stiff, pull, push = pl.pallas_call(
+        field_kernel,
+        out_shape=(plane(rows),) * 3,
+        in_specs=in_smem(2) + in_vmem(4),
+        out_specs=tuple(in_vmem(3)),
+        compiler_params=small,
+        name="field",
+    )(kl_coeff, across, along, tile_view(rigidity), tile_view(inv_mass), tile_view(gust_load))
+    wide = far - 1
+    low, high = exchanged(
+        jnp.concatenate([stiff[:wide], pull[:near], push[:near]]),
+        jnp.concatenate([stiff[rows - wide:], pull[rows - near:], push[rows - near:]]),
+        odd,
+    )
+    stiff = jnp.concatenate([low[:wide], stiff, high[:wide]])
+    pull = jnp.concatenate([low[wide:wide + near], pull, high[wide:wide + near]])
+    push = jnp.concatenate([low[wide + near:], push, high[wide + near:]])
+
+    first = time_slot == 0
+    edge = jnp.where(first, edge_own, edge_in)
+    mid = jnp.where(first, mid_own, mid_in)
+    low, high = exchanged(edge[:side], edge[side:2 * side], odd)
+    inside = rows - 2 * far
+    position = jnp.concatenate(
+        [low[:far], edge[:far], mid[:inside], edge[side:side + far], high[:far]]
+    )
+    velocity = jnp.concatenate(
+        [low[far:], edge[far:side], mid[inside:], edge[side + far:2 * side], high[far:]]
+    )
+    gusts = jnp.stack([edge[2 * side], edge_own[2 * side]])
+
+    out = pl.pallas_call(
+        functools.partial(chain_kernel, rows=rows, far=far),
+        out_shape=jax.ShapeDtypeStruct((2 * rows * SUBLANES, LANES), jnp.float32),
+        in_specs=in_smem(1) + in_vmem(6),
+        out_specs=in_vmem(1)[0],
+        scratch_shapes=[
+            pltpu.VMEM((rows + 2 * far, SUBLANES, LANES), jnp.float32),
+        ]
+        + [pltpu.VMEM((rows + 2 * near, SUBLANES, LANES), jnp.float32)] * 3,
+        compiler_params=small,
+        name="chain",
+    )(time_slot.reshape(1), position, velocity, stiff, pull, push, gusts)
+    return from_tile_view(out, start_state.shape)
+
+
+def chosen_device(start_state, rigidity, inv_mass, gust_load, kl_coeff, gust_history):
+    rows, cols = rigidity.shape
+    fits = cols == SUBLANES * LANES and rows % SUBLANES == 0 and rows > 4 * (2 * FINE + 1)
+    two_slices = lax.axis_size("tm") == 2 and ITERS == 2 and start_state.shape[0] == 1
+    device = two_slice_device if fits and two_slices else per_device
+    return device(start_state, rigidity, inv_mass, gust_load, kl_coeff, gust_history)
+
+
 def solution(mesh):
     in_specs = (
         P("tm", None, "space", None),
@@ -171,5 +480,5 @@
     )
     out_specs = P("tm", None, "space", None)
     return jax.shard_map(
-        per_device, mesh=mesh, in_specs=in_specs, out_specs=out_specs, check_vma=False
-    )
+        chosen_device, mesh=mesh, in_specs=in_specs, out_specs=out_specs, check_vma=False
+    )

time: 104 us -> 50.4 us (0.48)
  starting transfers between devices: 40.8 us -> 10.2 us
  other arithmetic: 22 us -> 0.56 us
  waiting for transfers between devices: 35.9 us -> 16.6 us
  Pallas kernels: 0 us -> 18.6 us
  matrix products: 3.02 us -> 0 us
  local copies, waits for them, and re-layouts: 1.62 us -> 3.69 us
    ppermute x12 -> x4, starting transfers between devices: 38.2 us -> 7.59 us  [the longest x2 6.78 us: exchanged(): lax.ppermute(jnp.where(odd, high_rows, low_rows), 'space', swap_pairs(cou...]
    pallas_call x0 -> x3, Pallas kernels: none -> 18.6 us  [the longest x1 16.9 us: two_slice_device(): pl.pallas_call(functools.partial(chain_kernel, rows=rows, far=far), out_s...]
    add x8 -> x0, other arithmetic: 12.2 us -> none  [per_device(): pos_now = pos_now + TIME_STEP * half_vel]
    ppermute x2, waiting for transfers between devices: 21.5 us -> 11.3 us  [passed_along(): return lax.ppermute(block, axis, route)]
    ppermute x12 -> x4, waiting for transfers between devices: 14.3 us -> 5.29 us  [the longest x2 5.29 us: exchanged(): lax.ppermute(jnp.where(odd, high_rows, low_rows), 'space', swap_pairs(cou...]
    another operation x8 -> x1, other arithmetic: 5.44 us -> 0.01 us  [two_slice_device(): gusts = jnp.stack([edge[2 * side], edge_own[2 * side]])]
    unnamed x10 -> x20, local copies, waits for them, and re-layouts: 0.02 us -> 3.6 us
    dot_general x2 -> x0, matrix products: 3.02 us -> none  [the longest x1 1.86 us: build_rigidity(): kl_field = jnp.dot(across.T, mixed, precision=lax.Precision.HIGHEST)]
  transfers between devices with their start and end apart: 14 -> 6, of which waited for: 5 -> 3; matrix products, arithmetic and copies ran while one was open for 4% -> 1% of each run, Pallas kernels for 0% -> 1%
where the time goes in v1:
time: 50.4 us; the launch traced here: 49.9 us
  Pallas kernels  18.6 us (37%)
  waiting for transfers between devices  16.6 us (33%)
  starting transfers between devices  10.2 us (20%)
  local copies, waits for them, and re-layouts  3.69 us (7%)
  other arithmetic  0.56 us (1%)
    pallas_call x1, Pallas kernels, two_slice_device(): pl.pallas_call(functools.partial(chain_kernel, rows=rows, far=far), out_s...  16.9 us
    ppermute x2, waiting for transfers between devices, passed_along(): return lax.ppermute(block, axis, route)  11.3 us
    ppermute x2, starting transfers between devices, exchanged(): lax.ppermute(jnp.where(odd, high_rows, low_rows), 'space', swap_pairs(cou...  6.78 us
    ppermute x2, waiting for transfers between devices, exchanged(): lax.ppermute(jnp.where(odd, high_rows, low_rows), 'space', swap_pairs(cou...  5.29 us
    unnamed x20, local copies, waits for them, and re-layouts  3.6 us
    ppermute x2, starting transfers between devices, passed_along(): return lax.ppermute(block, axis, route)  2.58 us
  transfers between devices with their start and end apart: 6, of which 3 were waited for; matrix products, arithmetic and copies ran while one was open for 1% of the time, Pallas kernels for 1%

profile of v1, /device:TPU:7, one launch (start us, length us, event | category | flops | bytes accessed | tf_op | source)
XLA Modules:
  0.0 49.9 jit_solution(4499795131614483433)
XLA Ops:
  0.0 0.1 multiply_cosine_fusion.1.across_ref
  0.2 0.1 multiply_cosine_fusion.along_ref
  0.3 0.0 copy-start.4
  0.3 0.7 %copy-done.4 = f32[4,4]{1,0:T(4,128)S(1)} copy-done((f32[4,4]{1,0:T(4,128)S(1)}, f32[4,4]{1,0:T(4,128)}, u32[]{:S(2)}) %copy-start.4) | copy-done | bytes 88
  1.0 0.0 copy-start.1
  1.0 0.9 %copy-done.1 = f32[64,1024]{1,0:T(8,128)S(1)} copy-done((f32[64,1024]{1,0:T(8,128)S(1)}, f32[64,1024]{1,0:T(8,128)}, u32[]{:S(2)}) %copy-start.1) | copy-done | bytes 262168
  1.9 0.0 copy-start.2
  1.9 0.9 %copy-done.2 = f32[64,1024]{1,0:T(8,128)S(1)} copy-done((f32[64,1024]{1,0:T(8,128)S(1)}, f32[64,1024]{1,0:T(8,128)}, u32[]{:S(2)}) %copy-start.2) | copy-done | bytes 262168
  2.9 0.0 copy-start.3
  2.9 0.9 %copy-done.3 = f32[64,1024]{1,0:T(8,128)S(1)} copy-done((f32[64,1024]{1,0:T(8,128)S(1)}, f32[64,1024]{1,0:T(8,128)}, u32[]{:S(2)}) %copy-start.3) | copy-done | bytes 262168
  3.8 1.0 %field.1 = (f32[64,8,128]{2,1,0:T(8,128)S(1)}, f32[64,8,128]{2,1,0:T(8,128)S(1)}, f32[64,8,128]{2,1,0:T(8,128)S(1)}) custom-call(f32[4,4]{1,0:T(4,128)S(1)} %copy-done.4, f32[4,64]{1,0:T(4,128)S(1)} %multiply_cosine_fusion.1.across_ref, f32[4,8,128]{2,1,0:T(8,128)S(1)} %multiply_cosine_fusion.along_ref, f32[512,128]{1,0:T(8,128)S(1)} %bitcast.27, ...), custom_call_target="tpu_custom_call" | custom-call | tf_op jit(solution)/shard_map/field/pallas_call | solution.py:418
  4.9 0.0 copy-start
  5.0 0.7 %collective-permute-start.4 = (f32[49,8,128]{2,1,0:T(8,128)S(1)}, f32[49,8,128]{2,1,0:T(8,128)S(1)}, u32[]{:S(2)}, u32[]{:S(2)}) collective-permute-start(f32[49,8,128]{2,1,0:T(8,128)S(1)} %get-tuple-element.17), channel_id=1, source_target_pairs={{0,1},{2,3},{4,5},{6,7},{8,9},{10,11},{12,13},{14,15},{1,0},{3,2},... | collective-permute-start | bytes 602120 | tf_op jit(solution)/shard_map/ppermute | solution.py:378
  5.7 0.0 copy-start.5
  5.7 3.2 %collective-permute-start.5 = (f32[49,8,128]{2,1,0:T(8,128)S(1)}, f32[49,8,128]{2,1,0:T(8,128)S(1)}, u32[]{:S(2)}, u32[]{:S(2)}) collective-permute-start(f32[49,8,128]{2,1,0:T(8,128)S(1)} %get-tuple-element.18), channel_id=1, source_target_pairs={{1,2},{3,4},{5,6},{7,8},{9,10},{11,12},{13,14},{2,1},{4,3},{6,5},{... | collective-permute-start | bytes 602120 | tf_op jit(solution)/shard_map/ppermute | solution.py:379
  8.9 0.0 copy-done
  8.9 0.0 copy-done.5
  8.9 0.6 %pack.1 = (f32[69,8,128]{2,1,0:T(8,128)S(1)}, f32[60,8,128]{2,1,0:T(8,128)S(1)}) custom-call(f32[4]{0:T(128)S(1)} %copy-done.5, f32[1024,128]{1,0:T(8,128)S(1)} %bitcast.26), custom_call_target="tpu_custom_call" | custom-call | tf_op jit(solution)/shard_map/pack/pallas_call | solution.py:405
  9.6 1.3 %collective-permute-start.3 = (f32[60,8,128]{2,1,0:T(8,128)S(1)}, f32[60,8,128]{2,1,0:T(8,128)S(1)}, u32[]{:S(2)}, u32[]{:S(2)}) collective-permute-start(f32[60,8,128]{2,1,0:T(8,128)S(1)} %get-tuple-element.11), channel_id=1, source_target_pairs={{0,16},{1,17},{2,18},{3,19},{4,20},{5,21},{6,22},{7,23},{8,24},{9,... | collective-permute-start | bytes 737288 | tf_op jit(solution)/shard_map/ppermute | solution.py:37
  10.9 1.3 %collective-permute-start = (f32[69,8,128]{2,1,0:T(8,128)S(1)}, f32[69,8,128]{2,1,0:T(8,128)S(1)}, u32[]{:S(2)}, u32[]{:S(2)}) collective-permute-start(f32[69,8,128]{2,1,0:T(8,128)S(1)} %get-tuple-element.10), channel_id=1, source_target_pairs={{0,16},{1,17},{2,18},{3,19},{4,20},{5,21},{6,22},{7,23},{8,24},{9,... | collective-permute-start | bytes 847880 | tf_op jit(solution)/shard_map/ppermute | solution.py:37
  12.2 0.0 collective-permute-done.4
  12.2 1.7 %collective-permute-done.5 = f32[49,8,128]{2,1,0:T(8,128)S(1)} collective-permute-done((f32[49,8,128]{2,1,0:T(8,128)S(1)}, f32[49,8,128]{2,1,0:T(8,128)S(1)}, u32[]{:S(2)}, u32[]{:S(2)}) %collective-permute-start.5) | collective-permute-done | bytes 200736 | tf_op jit(solution)/shard_map/ppermute | solution.py:379
  13.9 0.1 broadcast_select_fusion.3
  14.0 0.1 pad_maximum_fusion.1
  14.1 11.3 %collective-permute-done = f32[69,8,128]{2,1,0:T(8,128)S(1)} collective-permute-done((f32[69,8,128]{2,1,0:T(8,128)S(1)}, f32[69,8,128]{2,1,0:T(8,128)S(1)}, u32[]{:S(2)}, u32[]{:S(2)}) %collective-permute-start) | collective-permute-done | bytes 282656 | tf_op jit(solution)/shard_map/ppermute | solution.py:37
  25.4 3.6 %collective-permute-start.2 = (f32[34,8,128]{2,1,0:T(8,128)S(1)}, f32[34,8,128]{2,1,0:T(8,128)S(1)}, u32[]{:S(2)}, u32[]{:S(2)}) collective-permute-start(f32[34,8,128]{2,1,0:T(8,128)S(1)} %get-tuple-element.19), channel_id=1, source_target_pairs={{1,2},{3,4},{5,6},{7,8},{9,10},{11,12},{13,14},{2,1},{4,3},{6,5},{... | collective-permute-start | bytes 417800 | tf_op jit(solution)/shard_map/ppermute | solution.py:379
  29.0 0.1 collective-permute-start.1
  29.1 0.0 collective-permute-done.3
  29.2 3.6 %collective-permute-done.2 = f32[34,8,128]{2,1,0:T(8,128)S(1)} collective-permute-done((f32[34,8,128]{2,1,0:T(8,128)S(1)}, f32[34,8,128]{2,1,0:T(8,128)S(1)}, u32[]{:S(2)}, u32[]{:S(2)}) %collective-permute-start.2) | collective-permute-done | bytes 139296 | tf_op jit(solution)/shard_map/ppermute | solution.py:379
  32.8 0.0 collective-permute-done.1
  33.0 16.9 %chain.1 = f32[1024,128]{1,0:T(8,128)} custom-call(s32[1]{0:T(128)} %bitcast.slot_ref, f32[100,8,128]{2,1,0:T(8,128)S(1)} %slice_dynamic-update-slice_fusion.2.pos_in, f32[96,8,128]{2,1,0:T(8,128)S(1)} %slice_dynamic-update-slice_fusion.6.vel_in, f32[98,8,128]{2,1,0:T(8,128)S(1)} %pad_maximum_fusion.stiff_ref, f32[96,8,128]{2,1,0:T(8,128)S(1)} %get-tuple-element.33.pull_ref, ...), custom_call_target="tpu_custom_call" | custom-call | tf_op jit(solution)/shard_map/chain/pallas_call | solution.py:449
  (29 shorter events, 0.4 us)
Async XLA Ops:
  0.3 0.7 %copy-start.4 = (f32[4,4]{1,0:T(4,128)S(1)}, f32[4,4]{1,0:T(4,128)}, u32[]{:S(2)}) copy-start(f32[4,4]{1,0:T(4,128)} %kl_ref.1) | copy-start | bytes 196
  1.0 0.9 %copy-start.1 = (f32[64,1024]{1,0:T(8,128)S(1)}, f32[64,1024]{1,0:T(8,128)}, u32[]{:S(2)}) copy-start(f32[64,1024]{1,0:T(8,128)} %param.7) | copy-start | bytes 786436
  1.9 0.9 %copy-start.2 = (f32[64,1024]{1,0:T(8,128)S(1)}, f32[64,1024]{1,0:T(8,128)}, u32[]{:S(2)}) copy-start(f32[64,1024]{1,0:T(8,128)} %param.8) | copy-start | bytes 786436
  2.9 0.9 %copy-start.3 = (f32[64,1024]{1,0:T(8,128)S(1)}, f32[64,1024]{1,0:T(8,128)}, u32[]{:S(2)}) copy-start(f32[64,1024]{1,0:T(8,128)} %param.9) | copy-start | bytes 786436
  4.9 4.0 %copy-start = (f32[1,2,64,1024]{3,2,1,0:T(8,128)S(1)}, f32[1,2,64,1024]{3,2,1,0:T(8,128)}, u32[]{:S(2)}) copy-start(f32[1,2,64,1024]{3,2,1,0:T(8,128)} %param.6) | copy-start | bytes 1572868
  5.0 7.2 %collective-permute-start.4 = (f32[49,8,128]{2,1,0:T(8,128)S(1)}, f32[49,8,128]{2,1,0:T(8,128)S(1)}, u32[]{:S(2)}, u32[]{:S(2)}) collective-permute-start(f32[49,8,128]{2,1,0:T(8,128)S(1)} %get-tuple-element.17), channel_id=1, source_target_pairs={{0,1},{2,3},{4,5},{6,7},{8,9},{10,11},{12,13},{14,15},{1,0},{3,2},... | collective-permute-start | bytes 602120 | tf_op jit(solution)/shard_map/ppermute | solution.py:378
  5.7 3.2 %copy-start.5 = (f32[4]{0:T(128)S(1)}, f32[4]{0:T(128)}, u32[]{:S(2)}) copy-start(f32[4]{0:T(128)} %gust_ref.1) | copy-start | bytes 52
  5.7 8.2 %collective-permute-start.5 = (f32[49,8,128]{2,1,0:T(8,128)S(1)}, f32[49,8,128]{2,1,0:T(8,128)S(1)}, u32[]{:S(2)}, u32[]{:S(2)}) collective-permute-start(f32[49,8,128]{2,1,0:T(8,128)S(1)} %get-tuple-element.18), channel_id=1, source_target_pairs={{1,2},{3,4},{5,6},{7,8},{9,10},{11,12},{13,14},{2,1},{4,3},{6,5},{... | collective-permute-start | bytes 602120 | tf_op jit(solution)/shard_map/ppermute | solution.py:379
  9.6 19.5 %collective-permute-start.3 = (f32[60,8,128]{2,1,0:T(8,128)S(1)}, f32[60,8,128]{2,1,0:T(8,128)S(1)}, u32[]{:S(2)}, u32[]{:S(2)}) collective-permute-start(f32[60,8,128]{2,1,0:T(8,128)S(1)} %get-tuple-element.11), channel_id=1, source_target_pairs={{0,16},{1,17},{2,18},{3,19},{4,20},{5,21},{6,22},{7,23},{8,24},{9,... | collective-permute-start | bytes 737288 | tf_op jit(solution)/shard_map/ppermute | solution.py:37
  10.9 14.5 %collective-permute-start = (f32[69,8,128]{2,1,0:T(8,128)S(1)}, f32[69,8,128]{2,1,0:T(8,128)S(1)}, u32[]{:S(2)}, u32[]{:S(2)}) collective-permute-start(f32[69,8,128]{2,1,0:T(8,128)S(1)} %get-tuple-element.10), channel_id=1, source_target_pairs={{0,16},{1,17},{2,18},{3,19},{4,20},{5,21},{6,22},{7,23},{8,24},{9,... | collective-permute-start | bytes 847880 | tf_op jit(solution)/shard_map/ppermute | solution.py:37
  25.4 7.4 %collective-permute-start.2 = (f32[34,8,128]{2,1,0:T(8,128)S(1)}, f32[34,8,128]{2,1,0:T(8,128)S(1)}, u32[]{:S(2)}, u32[]{:S(2)}) collective-permute-start(f32[34,8,128]{2,1,0:T(8,128)S(1)} %get-tuple-element.19), channel_id=1, source_target_pairs={{1,2},{3,4},{5,6},{7,8},{9,10},{11,12},{13,14},{2,1},{4,3},{6,5},{... | collective-permute-start | bytes 417800 | tf_op jit(solution)/shard_map/ppermute | solution.py:379
  29.0 3.8 %collective-permute-start.1 = (f32[34,8,128]{2,1,0:T(8,128)S(1)}, f32[34,8,128]{2,1,0:T(8,128)S(1)}, u32[]{:S(2)}, u32[]{:S(2)}) collective-permute-start(f32[34,8,128]{2,1,0:T(8,128)S(1)} %get-tuple-element.20), channel_id=1, source_target_pairs={{0,1},{2,3},{4,5},{6,7},{8,9},{10,11},{12,13},{14,15},{1,0},{3,2},... | collective-permute-start | bytes 417800 | tf_op jit(solution)/shard_map/ppermute | solution.py:378

commit v2 on v1

--- a/solution.py
+++ b/solution.py
@@ -6,6 +6,7 @@
 from jax.experimental import pallas as pl
 from jax.experimental.pallas import tpu as pltpu
 from jax.sharding import PartitionSpec as P
+
 
 FINE = 4
 ITERS = 2
@@ -170,7 +171,7 @@
 DECAY = 1.0 - HALF_STEP * DAMPING
 COARSE_DECAY = 1.0 - COARSE_SPAN * DAMPING
 KICK = TIME_STEP * HALF_STEP
-UNROLL = 8
+UNROLL = 32
 
 
 def tile_view(block):
@@ -392,6 +393,32 @@
     return jax.ShapeDtypeStruct((count, SUBLANES, LANES), jnp.float32)
 
 
+def field_call(kl_coeff, across, along, rigidity, inv_mass, gust_load):
+    rows = rigidity.shape[0] // SUBLANES
+    return pl.pallas_call(
+        field_kernel,
+        out_shape=(plane(rows),) * 3,
+        in_specs=in_smem(2) + in_vmem(4),
+        out_specs=tuple(in_vmem(3)),
+        compiler_params=pltpu.CompilerParams(vmem_limit_bytes=16 * 2**20),
+        name="field",
+    )(kl_coeff, across, along, rigidity, inv_mass, gust_load)
+
+
+def chain_call(slot, position, velocity, stiff, pull, push, gusts, rows, far):
+    near = far - 2
+    return pl.pallas_call(
+        functools.partial(chain_kernel, rows=rows, far=far),
+        out_shape=jax.ShapeDtypeStruct((2 * rows * SUBLANES, LANES), jnp.float32),
+        in_specs=in_smem(1) + in_vmem(6),
+        out_specs=in_vmem(1)[0],
+        scratch_shapes=[pltpu.VMEM((rows + 2 * far, SUBLANES, LANES), jnp.float32)]
+        + [pltpu.VMEM((rows + 2 * near, SUBLANES, LANES), jnp.float32)] * 3,
+        compiler_params=pltpu.CompilerParams(vmem_limit_bytes=16 * 2**20),
+        name="chain",
+    )(slot, position, velocity, stiff, pull, push, gusts)
+
+
 def two_slice_device(start_state, rigidity, inv_mass, gust_load, kl_coeff, gust_history):
     rows, cols = rigidity.shape
     far = 2 * (2 * FINE + 1)
@@ -412,17 +439,15 @@
     )(gust_history, tile_view(start_state))
     edge_in = passed_along(edge_own, "tm", 1)
     mid_in = passed_along(mid_own, "tm", 1)
+    edge_own, rigidity, inv_mass, gust_load = lax.optimization_barrier(
+        (edge_own, rigidity, inv_mass, gust_load)
+    )
 
     across = mode_table(space_slot * rows + jnp.arange(rows), rows * lax.axis_size("space"))
     along = mode_table(jnp.arange(cols), cols).reshape(KL, SUBLANES, LANES)
-    stiff, pull, push = pl.pallas_call(
-        field_kernel,
-        out_shape=(plane(rows),) * 3,
-        in_specs=in_smem(2) + in_vmem(4),
-        out_specs=tuple(in_vmem(3)),
-        compiler_params=small,
-        name="field",
-    )(kl_coeff, across, along, tile_view(rigidity), tile_view(inv_mass), tile_view(gust_load))
+    stiff, pull, push = field_call(
+        kl_coeff, across, along, tile_view(rigidity), tile_view(inv_mass), tile_view(gust_load)
+    )
     wide = far - 1
     low, high = exchanged(
         jnp.concatenate([stiff[:wide], pull[:near], push[:near]]),
@@ -446,26 +471,21 @@
     )
     gusts = jnp.stack([edge[2 * side], edge_own[2 * side]])
 
-    out = pl.pallas_call(
-        functools.partial(chain_kernel, rows=rows, far=far),
-        out_shape=jax.ShapeDtypeStruct((2 * rows * SUBLANES, LANES), jnp.float32),
-        in_specs=in_smem(1) + in_vmem(6),
-        out_specs=in_vmem(1)[0],
-        scratch_shapes=[
-            pltpu.VMEM((rows + 2 * far, SUBLANES, LANES), jnp.float32),
-        ]
-        + [pltpu.VMEM((rows + 2 * near, SUBLANES, LANES), jnp.float32)] * 3,
-        compiler_params=small,
-        name="chain",
-    )(time_slot.reshape(1), position, velocity, stiff, pull, push, gusts)
+    out = chain_call(
+        time_slot.reshape(1), position, velocity, stiff, pull, push, gusts, rows, far
+    )
     return from_tile_view(out, start_state.shape)
+
+
+def layered_device(*args):
+    return two_slice_device(*args)
 
 
 def chosen_device(start_state, rigidity, inv_mass, gust_load, kl_coeff, gust_history):
     rows, cols = rigidity.shape
     fits = cols == SUBLANES * LANES and rows % SUBLANES == 0 and rows > 4 * (2 * FINE + 1)
     two_slices = lax.axis_size("tm") == 2 and ITERS == 2 and start_state.shape[0] == 1
-    device = two_slice_device if fits and two_slices else per_device
+    device = layered_device if fits and two_slices else per_device
     return device(start_state, rigidity, inv_mass, gust_load, kl_coeff, gust_history)
 
 

time: 50.4 us -> 36.7 us (0.73)
  Pallas kernels: 18.6 us -> 10.1 us
  waiting for transfers between devices: 16.6 us -> 10.8 us
    pallas_call x2, Pallas kernels: 17.9 us -> 9.42 us  [the longest x1 8.41 us: chain_call(): pl.pallas_call(functools.partial(chain_kernel, rows=rows, far=far), out_s...]
    ppermute x2, waiting for transfers between devices: 11.3 us -> 6.26 us  [passed_along(): return lax.ppermute(block, axis, route)]
    ppermute x2, waiting for transfers between devices: 5.29 us -> 4.52 us  [exchanged(): lax.ppermute(jnp.where(odd, high_rows, low_rows), 'space', swap_pairs(cou...]
    ppermute x2, starting transfers between devices: 6.78 us -> 7.31 us  [exchanged(): lax.ppermute(jnp.where(odd, high_rows, low_rows), 'space', swap_pairs(cou...]
  transfers between devices with their start and end apart: 6 -> 6, of which waited for: 3 -> 4; matrix products, arithmetic and copies ran while one was open for 1% -> 1% of each run, Pallas kernels for 1% -> 0%
where the time goes in v2:
time: 36.7 us; the launch traced here: 35.9 us
  waiting for transfers between devices  10.8 us (29%)
  starting transfers between devices  10.7 us (29%)
  Pallas kernels  10.1 us (28%)
  local copies, waits for them, and re-layouts  3.51 us (10%)
  other arithmetic  0.56 us (2%)
    pallas_call x1, Pallas kernels, chain_call(): pl.pallas_call(functools.partial(chain_kernel, rows=rows, far=far), out_s...  8.41 us
    ppermute x2, starting transfers between devices, exchanged(): lax.ppermute(jnp.where(odd, high_rows, low_rows), 'space', swap_pairs(cou...  7.31 us
    ppermute x2, waiting for transfers between devices, passed_along(): return lax.ppermute(block, axis, route)  6.26 us
    ppermute x2, waiting for transfers between devices, exchanged(): lax.ppermute(jnp.where(odd, high_rows, low_rows), 'space', swap_pairs(cou...  4.52 us
    unnamed x20, local copies, waits for them, and re-layouts  3.42 us
    ppermute x2, starting transfers between devices, passed_along(): return lax.ppermute(block, axis, route)  2.58 us
    pallas_call x1, Pallas kernels, field_call(): pl.pallas_call(field_kernel, out_shape=(plane(rows),) * 3, in_specs=in_sm...  1.01 us
    ppermute x2, starting transfers between devices, exchanged(): lax.ppermute(jnp.where(odd, low_rows, high_rows), 'space', swap_pairs(cou...  0.81 us
  transfers between devices with their start and end apart: 6, of which 4 were waited for; matrix products, arithmetic and copies ran while one was open for 1% of the time, Pallas kernels for 0%

profile of v2, /device:TPU:7, one launch (start us, length us, event | category | flops | bytes accessed | tf_op | source)
XLA Modules:
  0.0 35.9 jit_solution(2099832927256841593)
XLA Ops:
  0.0 0.1 multiply_cosine_fusion.1.across_ref
  0.2 0.1 multiply_cosine_fusion.along_ref
  0.3 0.0 copy-start.5
  0.3 0.6 %copy-done.5 = f32[4]{0:T(128)S(1)} copy-done((f32[4]{0:T(128)S(1)}, f32[4]{0:T(128)}, u32[]{:S(2)}) %copy-start.5) | copy-done | bytes 40
  1.0 0.0 copy-start
  1.0 1.0 %copy-done = f32[1,2,64,1024]{3,2,1,0:T(8,128)S(1)} copy-done((f32[1,2,64,1024]{3,2,1,0:T(8,128)S(1)}, f32[1,2,64,1024]{3,2,1,0:T(8,128)}, u32[]{:S(2)}) %copy-start) | copy-done | bytes 524312
  2.0 0.0 copy-start.1
  2.0 0.0 copy-start.2
  2.0 0.6 %pack.1 = (f32[69,8,128]{2,1,0:T(8,128)S(1)}, f32[60,8,128]{2,1,0:T(8,128)S(1)}) custom-call(f32[4]{0:T(128)S(1)} %copy-done.5, f32[1024,128]{1,0:T(8,128)S(1)} %bitcast.26), custom_call_target="tpu_custom_call" | custom-call | tf_op jit(solution)/shard_map/pack/pallas_call | solution.py:432
  2.7 0.0 copy-start.4
  2.7 0.3 copy-done.1
  2.9 0.1 copy-done.2
  3.0 0.3 copy-done.4
  3.4 0.0 copy-start.3
  3.4 0.9 %copy-done.3 = f32[64,1024]{1,0:T(8,128)S(1)} copy-done((f32[64,1024]{1,0:T(8,128)S(1)}, f32[64,1024]{1,0:T(8,128)}, u32[]{:S(2)}) %copy-start.3) | copy-done | bytes 262168
  4.3 1.0 %field.1 = (f32[64,8,128]{2,1,0:T(8,128)S(1)}, f32[64,8,128]{2,1,0:T(8,128)S(1)}, f32[64,8,128]{2,1,0:T(8,128)S(1)}) custom-call(f32[4,4]{1,0:T(4,128)S(1)} %copy-done.4, f32[4,64]{1,0:T(4,128)S(1)} %multiply_cosine_fusion.1.across_ref, f32[4,8,128]{2,1,0:T(8,128)S(1)} %multiply_cosine_fusion.along_ref, f32[512,128]{1,0:T(8,128)S(1)} %bitcast.27, ...), custom_call_target="tpu_custom_call" | custom-call | tf_op jit(solution)/shard_map/field/pallas_call | solution.py:398
  5.4 0.7 %collective-permute-start.4 = (f32[49,8,128]{2,1,0:T(8,128)S(1)}, f32[49,8,128]{2,1,0:T(8,128)S(1)}, u32[]{:S(2)}, u32[]{:S(2)}) collective-permute-start(f32[49,8,128]{2,1,0:T(8,128)S(1)} %get-tuple-element.25), channel_id=1, source_target_pairs={{0,1},{2,3},{4,5},{6,7},{8,9},{10,11},{12,13},{14,15},{1,0},{3,2},... | collective-permute-start | bytes 602120 | tf_op jit(solution)/shard_map/ppermute | solution.py:379
  6.2 3.0 %collective-permute-start.5 = (f32[49,8,128]{2,1,0:T(8,128)S(1)}, f32[49,8,128]{2,1,0:T(8,128)S(1)}, u32[]{:S(2)}, u32[]{:S(2)}) collective-permute-start(f32[49,8,128]{2,1,0:T(8,128)S(1)} %get-tuple-element.26), channel_id=1, source_target_pairs={{1,2},{3,4},{5,6},{7,8},{9,10},{11,12},{13,14},{2,1},{4,3},{6,5},{... | collective-permute-start | bytes 602120 | tf_op jit(solution)/shard_map/ppermute | solution.py:380
  9.2 1.3 %collective-permute-start = (f32[69,8,128]{2,1,0:T(8,128)S(1)}, f32[69,8,128]{2,1,0:T(8,128)S(1)}, u32[]{:S(2)}, u32[]{:S(2)}) collective-permute-start(f32[69,8,128]{2,1,0:T(8,128)S(1)} %get-tuple-element.15), channel_id=1, source_target_pairs={{0,16},{1,17},{2,18},{3,19},{4,20},{5,21},{6,22},{7,23},{8,24},{9,... | collective-permute-start | bytes 847880 | tf_op jit(solution)/shard_map/ppermute | solution.py:38
  10.5 1.3 %collective-permute-start.3 = (f32[60,8,128]{2,1,0:T(8,128)S(1)}, f32[60,8,128]{2,1,0:T(8,128)S(1)}, u32[]{:S(2)}, u32[]{:S(2)}) collective-permute-start(f32[60,8,128]{2,1,0:T(8,128)S(1)} %get-tuple-element.16), channel_id=1, source_target_pairs={{0,16},{1,17},{2,18},{3,19},{4,20},{5,21},{6,22},{7,23},{8,24},{9,... | collective-permute-start | bytes 737288 | tf_op jit(solution)/shard_map/ppermute | solution.py:38
  11.9 0.0 collective-permute-done.4
  11.9 2.3 %collective-permute-done.5 = f32[49,8,128]{2,1,0:T(8,128)S(1)} collective-permute-done((f32[49,8,128]{2,1,0:T(8,128)S(1)}, f32[49,8,128]{2,1,0:T(8,128)S(1)}, u32[]{:S(2)}, u32[]{:S(2)}) %collective-permute-start.5) | collective-permute-done | bytes 200736 | tf_op jit(solution)/shard_map/ppermute | solution.py:380
  14.2 0.1 broadcast_select_fusion.3
  14.4 0.1 pad_maximum_fusion.1
  14.4 5.5 %collective-permute-done = f32[69,8,128]{2,1,0:T(8,128)S(1)} collective-permute-done((f32[69,8,128]{2,1,0:T(8,128)S(1)}, f32[69,8,128]{2,1,0:T(8,128)S(1)}, u32[]{:S(2)}, u32[]{:S(2)}) %collective-permute-start) | collective-permute-done | bytes 282656 | tf_op jit(solution)/shard_map/ppermute | solution.py:38
  20.0 4.3 %collective-permute-start.2 = (f32[34,8,128]{2,1,0:T(8,128)S(1)}, f32[34,8,128]{2,1,0:T(8,128)S(1)}, u32[]{:S(2)}, u32[]{:S(2)}) collective-permute-start(f32[34,8,128]{2,1,0:T(8,128)S(1)} %get-tuple-element.27), channel_id=1, source_target_pairs={{1,2},{3,4},{5,6},{7,8},{9,10},{11,12},{13,14},{2,1},{4,3},{6,5},{... | collective-permute-start | bytes 417800 | tf_op jit(solution)/shard_map/ppermute | solution.py:380
  24.2 0.1 collective-permute-start.1
  24.3 0.8 %collective-permute-done.3 = f32[60,8,128]{2,1,0:T(8,128)S(1)} collective-permute-done((f32[60,8,128]{2,1,0:T(8,128)S(1)}, f32[60,8,128]{2,1,0:T(8,128)S(1)}, u32[]{:S(2)}, u32[]{:S(2)}) %collective-permute-start.3) | collective-permute-done | bytes 245792 | tf_op jit(solution)/shard_map/ppermute | solution.py:38
  25.1 2.2 %collective-permute-done.2 = f32[34,8,128]{2,1,0:T(8,128)S(1)} collective-permute-done((f32[34,8,128]{2,1,0:T(8,128)S(1)}, f32[34,8,128]{2,1,0:T(8,128)S(1)}, u32[]{:S(2)}, u32[]{:S(2)}) %collective-permute-start.2) | collective-permute-done | bytes 139296 | tf_op jit(solution)/shard_map/ppermute | solution.py:380
  27.3 0.0 collective-permute-done.1
  27.5 8.4 %chain.1 = f32[1024,128]{1,0:T(8,128)} custom-call(s32[1]{0:T(128)} %bitcast.slot_ref, f32[100,8,128]{2,1,0:T(8,128)S(1)} %slice_dynamic-update-slice_fusion.2.pos_in, f32[96,8,128]{2,1,0:T(8,128)S(1)} %slice_dynamic-update-slice_fusion.6.vel_in, f32[98,8,128]{2,1,0:T(8,128)S(1)} %pad_maximum_fusion.stiff_ref, f32[96,8,128]{2,1,0:T(8,128)S(1)} %get-tuple-element.41.pull_ref, ...), custom_call_target="tpu_custom_call" | custom-call | tf_op jit(solution)/shard_map/chain/pallas_call | solution.py:410
  (29 shorter events, 0.4 us)
Async XLA Ops:
  0.3 0.7 %copy-start.5 = (f32[4]{0:T(128)S(1)}, f32[4]{0:T(128)}, u32[]{:S(2)}) copy-start(f32[4]{0:T(128)} %gust_ref.1) | copy-start | bytes 52
  1.0 1.0 %copy-start = (f32[1,2,64,1024]{3,2,1,0:T(8,128)S(1)}, f32[1,2,64,1024]{3,2,1,0:T(8,128)}, u32[]{:S(2)}) copy-start(f32[1,2,64,1024]{3,2,1,0:T(8,128)} %param.6) | copy-start | bytes 1572868
  2.0 0.9 %copy-start.1 = (f32[64,1024]{1,0:T(8,128)S(1)}, f32[64,1024]{1,0:T(8,128)}, u32[]{:S(2)}) copy-start(f32[64,1024]{1,0:T(8,128)} %param.7) | copy-start | bytes 786436
  2.0 1.0 %copy-start.2 = (f32[64,1024]{1,0:T(8,128)S(1)}, f32[64,1024]{1,0:T(8,128)}, u32[]{:S(2)}) copy-start(f32[64,1024]{1,0:T(8,128)} %param.8) | copy-start | bytes 786436
  2.7 0.7 %copy-start.4 = (f32[4,4]{1,0:T(4,128)S(1)}, f32[4,4]{1,0:T(4,128)}, u32[]{:S(2)}) copy-start(f32[4,4]{1,0:T(4,128)} %kl_ref.1) | copy-start | bytes 196
  3.4 0.9 %copy-start.3 = (f32[64,1024]{1,0:T(8,128)S(1)}, f32[64,1024]{1,0:T(8,128)}, u32[]{:S(2)}) copy-start(f32[64,1024]{1,0:T(8,128)} %param.9) | copy-start | bytes 786436
  5.4 6.4 %collective-permute-start.4 = (f32[49,8,128]{2,1,0:T(8,128)S(1)}, f32[49,8,128]{2,1,0:T(8,128)S(1)}, u32[]{:S(2)}, u32[]{:S(2)}) collective-permute-start(f32[49,8,128]{2,1,0:T(8,128)S(1)} %get-tuple-element.25), channel_id=1, source_target_pairs={{0,1},{2,3},{4,5},{6,7},{8,9},{10,11},{12,13},{14,15},{1,0},{3,2},... | collective-permute-start | bytes 602120 | tf_op jit(solution)/shard_map/ppermute | solution.py:379
  6.2 8.0 %collective-permute-start.5 = (f32[49,8,128]{2,1,0:T(8,128)S(1)}, f32[49,8,128]{2,1,0:T(8,128)S(1)}, u32[]{:S(2)}, u32[]{:S(2)}) collective-permute-start(f32[49,8,128]{2,1,0:T(8,128)S(1)} %get-tuple-element.26), channel_id=1, source_target_pairs={{1,2},{3,4},{5,6},{7,8},{9,10},{11,12},{13,14},{2,1},{4,3},{6,5},{... | collective-permute-start | bytes 602120 | tf_op jit(solution)/shard_map/ppermute | solution.py:380
  9.2 10.7 %collective-permute-start = (f32[69,8,128]{2,1,0:T(8,128)S(1)}, f32[69,8,128]{2,1,0:T(8,128)S(1)}, u32[]{:S(2)}, u32[]{:S(2)}) collective-permute-start(f32[69,8,128]{2,1,0:T(8,128)S(1)} %get-tuple-element.15), channel_id=1, source_target_pairs={{0,16},{1,17},{2,18},{3,19},{4,20},{5,21},{6,22},{7,23},{8,24},{9,... | collective-permute-start | bytes 847880 | tf_op jit(solution)/shard_map/ppermute | solution.py:38
  10.5 14.6 %collective-permute-start.3 = (f32[60,8,128]{2,1,0:T(8,128)S(1)}, f32[60,8,128]{2,1,0:T(8,128)S(1)}, u32[]{:S(2)}, u32[]{:S(2)}) collective-permute-start(f32[60,8,128]{2,1,0:T(8,128)S(1)} %get-tuple-element.16), channel_id=1, source_target_pairs={{0,16},{1,17},{2,18},{3,19},{4,20},{5,21},{6,22},{7,23},{8,24},{9,... | collective-permute-start | bytes 737288 | tf_op jit(solution)/shard_map/ppermute | solution.py:38
  20.0 7.4 %collective-permute-start.2 = (f32[34,8,128]{2,1,0:T(8,128)S(1)}, f32[34,8,128]{2,1,0:T(8,128)S(1)}, u32[]{:S(2)}, u32[]{:S(2)}) collective-permute-start(f32[34,8,128]{2,1,0:T(8,128)S(1)} %get-tuple-element.27), channel_id=1, source_target_pairs={{1,2},{3,4},{5,6},{7,8},{9,10},{11,12},{13,14},{2,1},{4,3},{6,5},{... | collective-permute-start | bytes 417800 | tf_op jit(solution)/shard_map/ppermute | solution.py:380
  24.2 3.1 %collective-permute-start.1 = (f32[34,8,128]{2,1,0:T(8,128)S(1)}, f32[34,8,128]{2,1,0:T(8,128)S(1)}, u32[]{:S(2)}, u32[]{:S(2)}) collective-permute-start(f32[34,8,128]{2,1,0:T(8,128)S(1)} %get-tuple-element.28), channel_id=1, source_target_pairs={{0,1},{2,3},{4,5},{6,7},{8,9},{10,11},{12,13},{14,15},{1,0},{3,2},... | collective-permute-start | bytes 417800 | tf_op jit(solution)/shard_map/ppermute | solution.py:379

commit v3 on v2

--- a/solution.py
+++ b/solution.py
@@ -191,14 +191,22 @@
     return view_ref[pl.ds(start + row, SUBLANES, stride=SUBLANES), :]
 
 
-def pack_kernel(gust_ref, view_ref, edge_ref, mid_ref, *, rows, far, near):
-    sub = lax.broadcasted_iota(jnp.int32, (SUBLANES, LANES), 0)
-    gusts = jnp.zeros((SUBLANES, LANES), jnp.float32)
-    for step_index in range(FINE):
-        gusts = jnp.where(sub == step_index, gust_ref[step_index], gusts)
+def pack_kernel(
+    gust_hbm, view_hbm, edge_ref, mid_ref, view_ref, gust_ref, sems, *, rows, far, near
+):
+    gust_copy = pltpu.make_async_copy(gust_hbm, gust_ref, sems.at[2])
+    half = rows * SUBLANES
+    copies = []
+    for part in range(2):
+        piece = pl.ds(part * half, half)
+        copies.append(
+            pltpu.make_async_copy(view_hbm.at[piece], view_ref.at[piece], sems.at[part])
+        )
+        copies[part].start()
+    gust_copy.start()
     side = far + near
-    edge_ref[2 * side] = gusts
     for part, width, at in ((0, far, 0), (1, near, far)):
+        copies[part].wait()
         for row in range(rows):
             group = (part * rows + row) // SUBLANES
             value = row_at(view_ref, group, row % SUBLANES)
@@ -208,6 +216,12 @@
                 edge_ref[side + at + row - (rows - width)] = value
             else:
                 mid_ref[part * (rows - 2 * far) + row - width] = value
+    gust_copy.wait()
+    sub = lax.broadcasted_iota(jnp.int32, (SUBLANES, LANES), 0)
+    gusts = jnp.zeros((SUBLANES, LANES), jnp.float32)
+    for step_index in range(FINE):
+        gusts = jnp.where(sub == step_index, gust_ref[step_index], gusts)
+    edge_ref[2 * side] = gusts
 
 
 def field_kernel(
@@ -389,6 +403,10 @@
     return [pl.BlockSpec(memory_space=pltpu.SMEM)] * count
 
 
+def in_hbm(array):
+    return pltpu.with_memory_space_constraint(array, pltpu.HBM)
+
+
 def plane(count):
     return jax.ShapeDtypeStruct((count, SUBLANES, LANES), jnp.float32)
 
@@ -432,11 +450,16 @@
     edge_own, mid_own = pl.pallas_call(
         functools.partial(pack_kernel, rows=rows, far=far, near=near),
         out_shape=(plane(2 * side + 1), plane(2 * rows - 2 * side)),
-        in_specs=in_smem(1) + in_vmem(1),
+        in_specs=[pl.BlockSpec(memory_space=pltpu.HBM)] * 2,
         out_specs=tuple(in_vmem(2)),
+        scratch_shapes=[
+            pltpu.VMEM((2 * rows * SUBLANES, LANES), jnp.float32),
+            pltpu.SMEM((FINE,), jnp.float32),
+            pltpu.SemaphoreType.DMA((3,)),
+        ],
         compiler_params=small,
         name="pack",
-    )(gust_history, tile_view(start_state))
+    )(in_hbm(gust_history), in_hbm(tile_view(start_state)))
     edge_in = passed_along(edge_own, "tm", 1)
     mid_in = passed_along(mid_own, "tm", 1)
     edge_own, rigidity, inv_mass, gust_load = lax.optimization_barrier(

time: 36.7 us -> 35.4 us (0.965)
  local copies, waits for them, and re-layouts: 3.51 us -> 1.77 us
  Pallas kernels: 10.1 us -> 10.6 us
    unnamed x20 -> x16, local copies, waits for them, and re-layouts: 3.42 us -> 1.68 us
    pallas_call x1, Pallas kernels: 0.64 us -> 1.18 us  [two_slice_device(): pl.pallas_call(functools.partial(pack_kernel, rows=rows, far=far, near=ne...]
where the time goes in v3:
time: 35.4 us; the launch traced here: 34.8 us
  waiting for transfers between devices  10.8 us (31%)
  starting transfers between devices  10.7 us (30%)
  Pallas kernels  10.6 us (30%)
  local copies, waits for them, and re-layouts  1.77 us (5%)
  other arithmetic  0.56 us (2%)
    pallas_call x1, Pallas kernels, chain_call(): pl.pallas_call(functools.partial(chain_kernel, rows=rows, far=far), out_s...  8.41 us
    ppermute x2, starting transfers between devices, exchanged(): lax.ppermute(jnp.where(odd, high_rows, low_rows), 'space', swap_pairs(cou...  7.31 us
    ppermute x2, waiting for transfers between devices, passed_along(): return lax.ppermute(block, axis, route)  6.26 us
    ppermute x2, waiting for transfers between devices, exchanged(): lax.ppermute(jnp.where(odd, high_rows, low_rows), 'space', swap_pairs(cou...  4.52 us
    ppermute x2, starting transfers between devices, passed_along(): return lax.ppermute(block, axis, route)  2.58 us
    unnamed x16, local copies, waits for them, and re-layouts  1.68 us
    pallas_call x1, Pallas kernels, two_slice_device(): pl.pallas_call(functools.partial(pack_kernel, rows=rows, far=far, near=ne...  1.18 us
    pallas_call x1, Pallas kernels, field_call(): pl.pallas_call(field_kernel, out_shape=(plane(rows),) * 3, in_specs=in_sm...  1.01 us
  transfers between devices with their start and end apart: 6, of which 4 were waited for; matrix products, arithmetic and copies ran while one was open for 1% of the time, Pallas kernels for 0%

profile of v3, /device:TPU:7, one launch (start us, length us, event | category | flops | bytes accessed | tf_op | source)
XLA Modules:
  0.0 34.8 jit_solution(1070497068277059429)
XLA Ops:
  0.0 0.1 multiply_cosine_fusion.1.across_ref
  0.2 0.1 multiply_cosine_fusion.along_ref
  0.3 0.0 copy-start
  0.3 0.0 copy-start.1
  0.3 1.2 %pack.1 = (f32[69,8,128]{2,1,0:T(8,128)S(1)}, f32[60,8,128]{2,1,0:T(8,128)S(1)}) custom-call(f32[4]{0:T(128)} %gust_hbm.1, f32[1024,128]{1,0:T(8,128)} %bitcast.29), custom_call_target="tpu_custom_call" | custom-call | tf_op jit(solution)/shard_map/pack/pallas_call | solution.py:450
  1.5 0.0 copy-start.3
  1.5 0.0 copy-done
  1.5 0.0 copy-done.1
  1.5 0.7 %copy-done.3 = f32[4,4]{1,0:T(4,128)S(1)} copy-done((f32[4,4]{1,0:T(4,128)S(1)}, f32[4,4]{1,0:T(4,128)}, u32[]{:S(2)}) %copy-start.3) | copy-done | bytes 88
  2.2 0.0 copy-start.2
  2.2 0.9 %copy-done.2 = f32[64,1024]{1,0:T(8,128)S(1)} copy-done((f32[64,1024]{1,0:T(8,128)S(1)}, f32[64,1024]{1,0:T(8,128)}, u32[]{:S(2)}) %copy-start.2) | copy-done | bytes 262168
  3.1 1.0 %field.1 = (f32[64,8,128]{2,1,0:T(8,128)S(1)}, f32[64,8,128]{2,1,0:T(8,128)S(1)}, f32[64,8,128]{2,1,0:T(8,128)S(1)}) custom-call(f32[4,4]{1,0:T(4,128)S(1)} %copy-done.3, f32[4,64]{1,0:T(4,128)S(1)} %multiply_cosine_fusion.1.across_ref, f32[4,8,128]{2,1,0:T(8,128)S(1)} %multiply_cosine_fusion.along_ref, f32[512,128]{1,0:T(8,128)S(1)} %bitcast.26, ...), custom_call_target="tpu_custom_call" | custom-call | tf_op jit(solution)/shard_map/field/pallas_call | solution.py:416
  4.3 0.7 %collective-permute-start.4 = (f32[49,8,128]{2,1,0:T(8,128)S(1)}, f32[49,8,128]{2,1,0:T(8,128)S(1)}, u32[]{:S(2)}, u32[]{:S(2)}) collective-permute-start(f32[49,8,128]{2,1,0:T(8,128)S(1)} %get-tuple-element.25), channel_id=1, source_target_pairs={{0,1},{2,3},{4,5},{6,7},{8,9},{10,11},{12,13},{14,15},{1,0},{3,2},... | collective-permute-start | bytes 602120 | tf_op jit(solution)/shard_map/ppermute | solution.py:393
  5.0 3.0 %collective-permute-start.5 = (f32[49,8,128]{2,1,0:T(8,128)S(1)}, f32[49,8,128]{2,1,0:T(8,128)S(1)}, u32[]{:S(2)}, u32[]{:S(2)}) collective-permute-start(f32[49,8,128]{2,1,0:T(8,128)S(1)} %get-tuple-element.26), channel_id=1, source_target_pairs={{1,2},{3,4},{5,6},{7,8},{9,10},{11,12},{13,14},{2,1},{4,3},{6,5},{... | collective-permute-start | bytes 602120 | tf_op jit(solution)/shard_map/ppermute | solution.py:394
  8.1 1.3 %collective-permute-start = (f32[69,8,128]{2,1,0:T(8,128)S(1)}, f32[69,8,128]{2,1,0:T(8,128)S(1)}, u32[]{:S(2)}, u32[]{:S(2)}) collective-permute-start(f32[69,8,128]{2,1,0:T(8,128)S(1)} %get-tuple-element.15), channel_id=1, source_target_pairs={{0,16},{1,17},{2,18},{3,19},{4,20},{5,21},{6,22},{7,23},{8,24},{9,... | collective-permute-start | bytes 847880 | tf_op jit(solution)/shard_map/ppermute | solution.py:38
  9.3 1.3 %collective-permute-start.3 = (f32[60,8,128]{2,1,0:T(8,128)S(1)}, f32[60,8,128]{2,1,0:T(8,128)S(1)}, u32[]{:S(2)}, u32[]{:S(2)}) collective-permute-start(f32[60,8,128]{2,1,0:T(8,128)S(1)} %get-tuple-element.16), channel_id=1, source_target_pairs={{0,16},{1,17},{2,18},{3,19},{4,20},{5,21},{6,22},{7,23},{8,24},{9,... | collective-permute-start | bytes 737288 | tf_op jit(solution)/shard_map/ppermute | solution.py:38
  10.7 0.0 collective-permute-done.4
  10.7 2.3 %collective-permute-done.5 = f32[49,8,128]{2,1,0:T(8,128)S(1)} collective-permute-done((f32[49,8,128]{2,1,0:T(8,128)S(1)}, f32[49,8,128]{2,1,0:T(8,128)S(1)}, u32[]{:S(2)}, u32[]{:S(2)}) %collective-permute-start.5) | collective-permute-done | bytes 200736 | tf_op jit(solution)/shard_map/ppermute | solution.py:394
  13.0 0.1 broadcast_select_fusion.3
  13.2 0.1 pad_maximum_fusion.1
  13.2 5.5 %collective-permute-done = f32[69,8,128]{2,1,0:T(8,128)S(1)} collective-permute-done((f32[69,8,128]{2,1,0:T(8,128)S(1)}, f32[69,8,128]{2,1,0:T(8,128)S(1)}, u32[]{:S(2)}, u32[]{:S(2)}) %collective-permute-start) | collective-permute-done | bytes 282656 | tf_op jit(solution)/shard_map/ppermute | solution.py:38
  18.8 4.3 %collective-permute-start.2 = (f32[34,8,128]{2,1,0:T(8,128)S(1)}, f32[34,8,128]{2,1,0:T(8,128)S(1)}, u32[]{:S(2)}, u32[]{:S(2)}) collective-permute-start(f32[34,8,128]{2,1,0:T(8,128)S(1)} %get-tuple-element.27), channel_id=1, source_target_pairs={{1,2},{3,4},{5,6},{7,8},{9,10},{11,12},{13,14},{2,1},{4,3},{6,5},{... | collective-permute-start | bytes 417800 | tf_op jit(solution)/shard_map/ppermute | solution.py:394
  23.0 0.1 collective-permute-start.1
  23.1 0.8 %collective-permute-done.3 = f32[60,8,128]{2,1,0:T(8,128)S(1)} collective-permute-done((f32[60,8,128]{2,1,0:T(8,128)S(1)}, f32[60,8,128]{2,1,0:T(8,128)S(1)}, u32[]{:S(2)}, u32[]{:S(2)}) %collective-permute-start.3) | collective-permute-done | bytes 245792 | tf_op jit(solution)/shard_map/ppermute | solution.py:38
  24.0 2.2 %collective-permute-done.2 = f32[34,8,128]{2,1,0:T(8,128)S(1)} collective-permute-done((f32[34,8,128]{2,1,0:T(8,128)S(1)}, f32[34,8,128]{2,1,0:T(8,128)S(1)}, u32[]{:S(2)}, u32[]{:S(2)}) %collective-permute-start.2) | collective-permute-done | bytes 139296 | tf_op jit(solution)/shard_map/ppermute | solution.py:394
  26.2 0.0 collective-permute-done.1
  26.3 8.4 %chain.1 = f32[1024,128]{1,0:T(8,128)} custom-call(s32[1]{0:T(128)} %bitcast.slot_ref, f32[100,8,128]{2,1,0:T(8,128)S(1)} %slice_dynamic-update-slice_fusion.2.pos_in, f32[96,8,128]{2,1,0:T(8,128)S(1)} %slice_dynamic-update-slice_fusion.6.vel_in, f32[98,8,128]{2,1,0:T(8,128)S(1)} %pad_maximum_fusion.stiff_ref, f32[96,8,128]{2,1,0:T(8,128)S(1)} %get-tuple-element.41.pull_ref, ...), custom_call_target="tpu_custom_call" | custom-call | tf_op jit(solution)/shard_map/chain/pallas_call | solution.py:428
  (29 shorter events, 0.4 us)
Async XLA Ops:
  0.3 1.2 %copy-start = (f32[64,1024]{1,0:T(8,128)S(1)}, f32[64,1024]{1,0:T(8,128)}, u32[]{:S(2)}) copy-start(f32[64,1024]{1,0:T(8,128)} %param.7) | copy-start | bytes 786436
  0.3 1.2 %copy-start.1 = (f32[64,1024]{1,0:T(8,128)S(1)}, f32[64,1024]{1,0:T(8,128)}, u32[]{:S(2)}) copy-start(f32[64,1024]{1,0:T(8,128)} %param.8) | copy-start | bytes 786436
  1.5 0.7 %copy-start.3 = (f32[4,4]{1,0:T(4,128)S(1)}, f32[4,4]{1,0:T(4,128)}, u32[]{:S(2)}) copy-start(f32[4,4]{1,0:T(4,128)} %kl_ref.1) | copy-start | bytes 196
  2.2 0.9 %copy-start.2 = (f32[64,1024]{1,0:T(8,128)S(1)}, f32[64,1024]{1,0:T(8,128)}, u32[]{:S(2)}) copy-start(f32[64,1024]{1,0:T(8,128)} %param.9) | copy-start | bytes 786436
  4.3 6.4 %collective-permute-start.4 = (f32[49,8,128]{2,1,0:T(8,128)S(1)}, f32[49,8,128]{2,1,0:T(8,128)S(1)}, u32[]{:S(2)}, u32[]{:S(2)}) collective-permute-start(f32[49,8,128]{2,1,0:T(8,128)S(1)} %get-tuple-element.25), channel_id=1, source_target_pairs={{0,1},{2,3},{4,5},{6,7},{8,9},{10,11},{12,13},{14,15},{1,0},{3,2},... | collective-permute-start | bytes 602120 | tf_op jit(solution)/shard_map/ppermute | solution.py:393
  5.0 8.0 %collective-permute-start.5 = (f32[49,8,128]{2,1,0:T(8,128)S(1)}, f32[49,8,128]{2,1,0:T(8,128)S(1)}, u32[]{:S(2)}, u32[]{:S(2)}) collective-permute-start(f32[49,8,128]{2,1,0:T(8,128)S(1)} %get-tuple-element.26), channel_id=1, source_target_pairs={{1,2},{3,4},{5,6},{7,8},{9,10},{11,12},{13,14},{2,1},{4,3},{6,5},{... | collective-permute-start | bytes 602120 | tf_op jit(solution)/shard_map/ppermute | solution.py:394
  8.1 10.7 %collective-permute-start = (f32[69,8,128]{2,1,0:T(8,128)S(1)}, f32[69,8,128]{2,1,0:T(8,128)S(1)}, u32[]{:S(2)}, u32[]{:S(2)}) collective-permute-start(f32[69,8,128]{2,1,0:T(8,128)S(1)} %get-tuple-element.15), channel_id=1, source_target_pairs={{0,16},{1,17},{2,18},{3,19},{4,20},{5,21},{6,22},{7,23},{8,24},{9,... | collective-permute-start | bytes 847880 | tf_op jit(solution)/shard_map/ppermute | solution.py:38
  9.3 14.6 %collective-permute-start.3 = (f32[60,8,128]{2,1,0:T(8,128)S(1)}, f32[60,8,128]{2,1,0:T(8,128)S(1)}, u32[]{:S(2)}, u32[]{:S(2)}) collective-permute-start(f32[60,8,128]{2,1,0:T(8,128)S(1)} %get-tuple-element.16), channel_id=1, source_target_pairs={{0,16},{1,17},{2,18},{3,19},{4,20},{5,21},{6,22},{7,23},{8,24},{9,... | collective-permute-start | bytes 737288 | tf_op jit(solution)/shard_map/ppermute | solution.py:38
  18.8 7.4 %collective-permute-start.2 = (f32[34,8,128]{2,1,0:T(8,128)S(1)}, f32[34,8,128]{2,1,0:T(8,128)S(1)}, u32[]{:S(2)}, u32[]{:S(2)}) collective-permute-start(f32[34,8,128]{2,1,0:T(8,128)S(1)} %get-tuple-element.27), channel_id=1, source_target_pairs={{1,2},{3,4},{5,6},{7,8},{9,10},{11,12},{13,14},{2,1},{4,3},{6,5},{... | collective-permute-start | bytes 417800 | tf_op jit(solution)/shard_map/ppermute | solution.py:394
  23.0 3.1 %collective-permute-start.1 = (f32[34,8,128]{2,1,0:T(8,128)S(1)}, f32[34,8,128]{2,1,0:T(8,128)S(1)}, u32[]{:S(2)}, u32[]{:S(2)}) collective-permute-start(f32[34,8,128]{2,1,0:T(8,128)S(1)} %get-tuple-element.28), channel_id=1, source_target_pairs={{0,1},{2,3},{4,5},{6,7},{8,9},{10,11},{12,13},{14,15},{1,0},{3,2},... | collective-permute-start | bytes 417800 | tf_op jit(solution)/shard_map/ppermute | solution.py:393

commit v4 on v3

--- a/solution.py
+++ b/solution.py
@@ -225,8 +225,24 @@
 
 
 def field_kernel(
-    kl_ref, across_ref, along_ref, rigid_ref, mass_ref, load_ref, stiff_ref, pull_ref, push_ref
+    across_ref, along_ref, kl_hbm, rigid_hbm, mass_hbm, load_hbm, stiff_ref, pull_ref, push_ref,
+    kl_ref, rigid_ref, mass_ref, load_ref, sems
 ):
+    copies = [
+        pltpu.make_async_copy(source, target, sems.at[at])
+        for at, (source, target) in enumerate(
+            (
+                (kl_hbm, kl_ref),
+                (rigid_hbm, rigid_ref),
+                (mass_hbm, mass_ref),
+                (load_hbm, load_ref),
+            )
+        )
+    ]
+    for copy in copies:
+        copy.start()
+    for copy in copies:
+        copy.wait()
     rows = stiff_ref.shape[0]
     mixed = []
     for order in range(KL):
@@ -250,137 +266,178 @@
     lax.fori_loop(0, rows // SUBLANES, group_rows, 0)
 
 
-def chain_kernel(
-    slot_ref, pos_in, vel_in, stiff_ref, pull_ref, push_ref, gust_ref, out_ref,
-    pos, vel, coarse_pos, coarse_vel, *, rows, far
-):
-    near = far - 2
+def beside(row):
     lane = lax.broadcasted_iota(jnp.int32, (SUBLANES, LANES), 1)
     sub = lax.broadcasted_iota(jnp.int32, (SUBLANES, LANES), 0)
     last_lane = lane == LANES - 1
     first_lane = lane == 0
-    low_corner = last_lane & (sub == 0)
-    high_corner = first_lane & (sub == SUBLANES - 1)
-    half_pull = 1.0 / (1.0 + DECAY)
-    slot = slot_ref[0]
-
-    def gust(stage, step_index):
-        return jnp.broadcast_to(gust_ref[stage, step_index:step_index + 1, :], (SUBLANES, LANES))
-
-    def beside(row):
-        below = jnp.where(last_lane, pltpu.roll(row, 1, 0), row)
-        above = jnp.where(first_lane, pltpu.roll(row, SUBLANES - 1, 0), row)
-        below = jnp.where(low_corner, 0.0, below)
-        above = jnp.where(high_corner, 0.0, above)
-        return pltpu.roll(below, 1, 1) + pltpu.roll(above, LANES - 1, 1)
-
-    def sweep(source, margin, update):
-        count = -(-(rows + 2 * margin) // UNROLL) * UNROLL
-        first = min(-margin, rows + near - count)
-
-        def weigh(row, before, here, after):
-            return stiff_ref[row + far - 1] * (before + after + beside(here) - 4.0 * here)
-
-        start = [source[first - 2 + far + i] for i in range(4)]
-        carry = (
-            weigh(first - 1, start[0], start[1], start[2]),
-            weigh(first, start[1], start[2], start[3]),
-            start[2],
-            start[3],
-        )
-
-        def chunk(index, carry):
-            base = first + index * UNROLL
-            w_before, w_here, p_here, p_after = carry
-            for j in range(UNROLL):
-                p_next = source[base + j + 2 + far]
-                w_after = weigh(base + j + 1, p_here, p_after, p_next)
-                bent = w_before + w_after + beside(w_here) - 4.0 * w_here
-                update(index, j, base + j, p_here, bent)
-                w_before, w_here, p_here, p_after = w_here, w_after, p_after, p_next
-            return w_before, w_here, p_here, p_after
-
-        lax.fori_loop(0, count // UNROLL, chunk, carry)
-
-    def start_slice(row, position, velocity, bent, gust_value):
-        force = gust_value * push_ref[row + near] - half_pull * (pull_ref[row + near] * bent)
-        shift = (TIME_STEP * DECAY) * velocity + force
-        new_vel = COARSE_DECAY * velocity + (COARSE_SPAN / KICK) * force
-        coarse_vel[row + near] = new_vel
-        coarse_pos[row + near] = position + COARSE_SPAN * new_vel
-        vel[row + near] = shift
-        pos[row + far] = position + shift
-
-    def advance(gust_value, joins):
-        def update(index, j, row, position, bent):
-            shift = (
-                (DECAY * DECAY) * vel[row + near]
-                + gust_value * push_ref[row + near]
-                - pull_ref[row + near] * bent
+    below = jnp.where(last_lane, pltpu.roll(row, 1, 0), row)
+    above = jnp.where(first_lane, pltpu.roll(row, SUBLANES - 1, 0), row)
+    below = jnp.where(last_lane & (sub == 0), 0.0, below)
+    above = jnp.where(first_lane & (sub == SUBLANES - 1), 0.0, above)
+    return pltpu.roll(below, 1, 1) + pltpu.roll(above, LANES - 1, 1)
+
+
+def splat(value):
+    return jnp.full((SUBLANES, LANES), value, jnp.float32)
+
+
+def gust_row(gust_ref, step_index):
+    stage, at = divmod(step_index, FINE)
+    return jnp.broadcast_to(gust_ref[stage, at:at + 1, :], (SUBLANES, LANES))
+
+
+HALF_PULL = 1.0 / (1.0 + DECAY)
+
+
+def fill_coef(coef, gust_ref, slot):
+    for index in range(2 * FINE + 1):
+        if index == 0:
+            terms = splat(DECAY * TIME_STEP), gust_row(gust_ref, 0), splat(HALF_PULL)
+        elif index == 2 * FINE:
+            terms = (
+                splat(DECAY / TIME_STEP),
+                gust_row(gust_ref, index - 1) / TIME_STEP,
+                splat(HALF_PULL / TIME_STEP),
             )
-            vel[row + near] = shift
-            moved = position + shift
-            if joins:
-                coarse = coarse_pos[row + near]
-                moved = coarse + (moved - coarse)
-            pos[row + far] = moved
-
-        return update
-
-    def end_velocity(row, bent, gust_value):
-        force = gust_value * push_ref[row + near] - half_pull * (pull_ref[row + near] * bent)
-        fine_vel = (1.0 / TIME_STEP) * (DECAY * vel[row + near] + force)
-        coarse = coarse_vel[row + near]
-        return coarse + (fine_vel - coarse)
-
-    def finish(gust_value):
-        def update(index, j, row, position, bent):
-            group = index * (UNROLL // SUBLANES) + j // SUBLANES
-            start = pl.multiple_of(group * SUBLANES * SUBLANES, SUBLANES * SUBLANES)
-            at = start + j % SUBLANES
-            out_ref[pl.ds(at, SUBLANES, stride=SUBLANES), :] = position
-            out_ref[pl.ds(at + rows * SUBLANES, SUBLANES, stride=SUBLANES), :] = end_velocity(
-                row, bent, gust_value
-            )
-
-        return update
-
-    def fine_steps(stage, margin):
-        for step_index in range(1, FINE):
-            gust_value = DECAY * gust(stage, step_index - 1) + gust(stage, step_index)
-            margin -= 2
-            sweep(pos, margin, advance(gust_value, step_index == FINE - 1))
-        return margin
-
-    blank = jnp.zeros((SUBLANES, LANES), jnp.float32)
-    for row in (-far, -far + 1, rows + far - 2, rows + far - 1):
-        pos[row + far] = blank
-    first_gust = gust(0, 0)
-    sweep(
-        pos_in,
-        near,
-        lambda index, j, row, position, bent: start_slice(
-            row, position, vel_in[row + near], bent, first_gust
-        ),
-    )
-    margin = fine_steps(0, near) - 2
+        else:
+            both = DECAY * gust_row(gust_ref, index - 1) + gust_row(gust_ref, index)
+            terms = splat(DECAY * DECAY), both, splat(1.0)
+        for at, term in enumerate(terms):
+            coef[index, at] = term
 
     @pl.when(slot == 0)
     def _():
-        sweep(pos, 0, finish(gust(0, FINE - 1)))
-
-    @pl.when(slot != 0)
+        coef[FINE, 0] = splat(DECAY / TIME_STEP)
+        coef[FINE, 1] = gust_row(gust_ref, FINE - 1) / TIME_STEP
+        coef[FINE, 2] = splat(HALF_PULL / TIME_STEP)
+
+
+def advance_rows(sweep, start, count, offset, pos, vel, coef, stiff_ref, pull_ref, push_ref):
+    here = [pos[sweep, start - 2 + i] for i in range(count + 4)]
+    sides = [beside(here[i]) for i in range(1, count + 3)]
+    weighted = [
+        stiff_ref[start - 1 + i - offset]
+        * (here[i] + here[i + 2] + sides[i] - 4.0 * here[i + 1])
+        for i in range(count + 2)
+    ]
+    alpha, push_by, pull_by = (coef[sweep, i] for i in range(3))
+    moved = []
+    for i in range(count):
+        row = start + i
+        bent = weighted[i] + weighted[i + 2] + beside(weighted[i + 1]) - 4.0 * weighted[i + 1]
+        shift = (
+            alpha * vel[sweep, row]
+            + push_by * push_ref[row - offset]
+            - pull_by * (pull_ref[row - offset] * bent)
+        )
+        moved.append((row, here[i + 2] + shift, shift))
+    return moved
+
+
+def keep_rows(sweep, moved, pos, vel):
+    for row, position, shift in moved:
+        pos[sweep + 1, row] = position
+        vel[sweep + 1, row] = shift
+
+
+def inner_kernel(
+    slot_ref, edge_ref, mid_ref, stiff_ref, pull_ref, push_ref, gust_ref, pos, vel, coef,
+    *, rows, far
+):
+    near = far - 2
+    side = far + near
+    top = far + 2
+    slot = slot_ref[0]
+    fill_coef(coef, gust_ref, slot)
+    inside = rows - 2 * far
+    for plane_ref, width, at, first in ((pos, far, 0, 0), (vel, near, far, inside)):
+        for i in range(width):
+            plane_ref[0, top + i] = edge_ref[at + i]
+            plane_ref[0, top + rows - width + i] = edge_ref[side + at + i]
+        for i in range(rows - 2 * width):
+            plane_ref[0, top + width + i] = mid_ref[first + i]
+
+    def sweep_all(sweep, carry):
+        first = 2 * sweep + 2
+        end = rows - first
+
+        def chunk(index, carry):
+            start = jnp.minimum(first + index * UNROLL, end - UNROLL) + top
+            moved = advance_rows(
+                sweep, start, UNROLL, top, pos, vel, coef, stiff_ref, pull_ref, push_ref
+            )
+            keep_rows(sweep, moved, pos, vel)
+            return carry
+
+        return lax.fori_loop(0, (end - first + UNROLL - 1) // UNROLL, chunk, carry)
+
+    lax.fori_loop(0, jnp.where(slot == 0, FINE + 1, 2 * FINE + 1), sweep_all, 0)
+
+
+def outer_kernel(
+    slot_ref, odd_ref, inner_halo, outer_halo, stiff_ref, pull_ref, push_ref, gust_ref, pos_in,
+    vel_in, pos, vel, out_ref, coef, *, rows, far
+):
+    near = far - 2
+    top = far + 2
+    slot = slot_ref[0]
+    sweeps = jnp.where(slot == 0, FINE + 1, 2 * FINE + 1)
+    fill_coef(coef, gust_ref, slot)
+
+    def fill_halo(low, high):
+        for i in range(far):
+            pos[0, top - far + i] = low[i]
+            pos[0, top + rows + i] = high[i]
+        for i in range(near):
+            vel[0, top - near + i] = low[far + i]
+            vel[0, top + rows + i] = high[far + i]
+
+    @pl.when(odd_ref[0] == 0)
     def _():
-        last_gust = gust(0, FINE - 1)
-        next_gust = gust(1, 0)
-
-        def link(index, j, row, position, bent):
-            velocity = end_velocity(row, bent, last_gust)
-            start_slice(row, position, velocity, bent, next_gust)
-
-        sweep(pos, margin, link)
-        fine_steps(1, margin)
-        sweep(pos, 0, finish(gust(1, FINE - 1)))
+        fill_halo(outer_halo, inner_halo)
+
+    @pl.when(odd_ref[0] != 0)
+    def _():
+        fill_halo(inner_halo, outer_halo)
+
+    def sweep_all(sweep, carry):
+        moved = []
+        for start in (top - near + 2 * sweep, top + rows - 2 - 2 * sweep):
+            moved += advance_rows(
+                sweep, start, far, 0, pos, vel, coef, stiff_ref, pull_ref, push_ref
+            )
+        keep_rows(sweep, moved, pos, vel)
+        return carry
+
+    lax.fori_loop(0, sweeps, sweep_all, 0)
+
+    begin = slot * FINE
+    own = slot == 0
+    by_start = splat(jnp.where(own, TIME_STEP, DECAY * HALF_PULL))
+    by_next = splat(jnp.where(own, 0.0, HALF_PULL))
+    gust_step = gust_row(gust_ref, FINE - 1) - gust_row(gust_ref, FINE)
+    by_push = jnp.where(own, 0.0, HALF_PULL) * gust_step
+
+    def finish(group, carry):
+        first = pl.multiple_of(group * SUBLANES * SUBLANES, SUBLANES * SUBLANES)
+        for j in range(SUBLANES):
+            row = group * SUBLANES + j + top
+            following = vel[begin + 1, row]
+            scaled = by_start * vel[begin, row] + by_next * following + by_push * push_ref[row]
+            force = following - DECAY * scaled
+            coarse_vel = (COARSE_DECAY / TIME_STEP) * scaled + (COARSE_SPAN / KICK) * force
+            coarse_pos = pos[begin, row] + COARSE_SPAN * coarse_vel
+            delta_pos = pos[sweeps - 1, row] - coarse_pos
+            delta_vel = vel[sweeps, row] - coarse_vel
+            at = first + j
+            out_ref[pl.ds(at, SUBLANES, stride=SUBLANES), :] = coarse_pos + delta_pos
+            out_ref[pl.ds(at + rows * SUBLANES, SUBLANES, stride=SUBLANES), :] = (
+                coarse_vel + delta_vel
+            )
+        return carry
+
+    lax.fori_loop(0, rows // SUBLANES, finish, 0)
 
 
 def swap_pairs(count, first):
@@ -392,7 +449,7 @@
     count = lax.axis_size("space")
     inner = lax.ppermute(jnp.where(odd, low_rows, high_rows), "space", swap_pairs(count, 0))
     outer = lax.ppermute(jnp.where(odd, high_rows, low_rows), "space", swap_pairs(count, 1))
-    return jnp.where(odd, inner, outer), jnp.where(odd, outer, inner)
+    return inner, outer
 
 
 def in_vmem(count):
@@ -411,30 +468,62 @@
     return jax.ShapeDtypeStruct((count, SUBLANES, LANES), jnp.float32)
 
 
-def field_call(kl_coeff, across, along, rigidity, inv_mass, gust_load):
+def field_call(across, along, kl_coeff, rigidity, inv_mass, gust_load):
     rows = rigidity.shape[0] // SUBLANES
     return pl.pallas_call(
         field_kernel,
         out_shape=(plane(rows),) * 3,
-        in_specs=in_smem(2) + in_vmem(4),
+        in_specs=in_smem(1) + in_vmem(1) + [pl.BlockSpec(memory_space=pltpu.HBM)] * 4,
         out_specs=tuple(in_vmem(3)),
+        scratch_shapes=[pltpu.SMEM((KL, KL), jnp.float32)]
+        + [pltpu.VMEM(rigidity.shape, jnp.float32)] * 3
+        + [pltpu.SemaphoreType.DMA((4,))],
         compiler_params=pltpu.CompilerParams(vmem_limit_bytes=16 * 2**20),
         name="field",
-    )(kl_coeff, across, along, rigidity, inv_mass, gust_load)
-
-
-def chain_call(slot, position, velocity, stiff, pull, push, gusts, rows, far):
-    near = far - 2
+    )(
+        across,
+        along,
+        in_hbm(kl_coeff),
+        in_hbm(rigidity),
+        in_hbm(inv_mass),
+        in_hbm(gust_load),
+    )
+
+
+def state_planes(rows, far):
+    shape = (2 * FINE + 2, rows + 2 * far + 4, SUBLANES, LANES)
+    return jax.ShapeDtypeStruct(shape, jnp.float32)
+
+
+def coef_scratch():
+    return [pltpu.VMEM((2 * FINE + 1, 3, SUBLANES, LANES), jnp.float32)]
+
+
+def inner_call(slot, edge, mid, stiff, pull, push, gusts, rows, far):
     return pl.pallas_call(
-        functools.partial(chain_kernel, rows=rows, far=far),
-        out_shape=jax.ShapeDtypeStruct((2 * rows * SUBLANES, LANES), jnp.float32),
+        functools.partial(inner_kernel, rows=rows, far=far),
+        out_shape=(state_planes(rows, far),) * 2,
         in_specs=in_smem(1) + in_vmem(6),
-        out_specs=in_vmem(1)[0],
-        scratch_shapes=[pltpu.VMEM((rows + 2 * far, SUBLANES, LANES), jnp.float32)]
-        + [pltpu.VMEM((rows + 2 * near, SUBLANES, LANES), jnp.float32)] * 3,
-        compiler_params=pltpu.CompilerParams(vmem_limit_bytes=16 * 2**20),
-        name="chain",
-    )(slot, position, velocity, stiff, pull, push, gusts)
+        out_specs=tuple(in_vmem(2)),
+        scratch_shapes=coef_scratch(),
+        compiler_params=pltpu.CompilerParams(vmem_limit_bytes=24 * 2**20),
+        name="inner",
+    )(slot, edge, mid, stiff, pull, push, gusts)
+
+
+def outer_call(slot, odd, inner, outer, stiff, pull, push, gusts, pos, vel, rows, far):
+    planes = state_planes(rows, far)
+    out = jax.ShapeDtypeStruct((2 * rows * SUBLANES, LANES), jnp.float32)
+    return pl.pallas_call(
+        functools.partial(outer_kernel, rows=rows, far=far),
+        out_shape=(planes, planes, out),
+        in_specs=in_smem(2) + in_vmem(8),
+        out_specs=tuple(in_vmem(3)),
+        scratch_shapes=coef_scratch(),
+        input_output_aliases={8: 0, 9: 1},
+        compiler_params=pltpu.CompilerParams(vmem_limit_bytes=24 * 2**20),
+        name="outer",
+    )(slot, odd, inner, outer, stiff, pull, push, gusts, pos, vel)[2]
 
 
 def two_slice_device(start_state, rigidity, inv_mass, gust_load, kl_coeff, gust_history):
@@ -469,33 +558,37 @@
     across = mode_table(space_slot * rows + jnp.arange(rows), rows * lax.axis_size("space"))
     along = mode_table(jnp.arange(cols), cols).reshape(KL, SUBLANES, LANES)
     stiff, pull, push = field_call(
-        kl_coeff, across, along, tile_view(rigidity), tile_view(inv_mass), tile_view(gust_load)
+        across, along, kl_coeff, tile_view(rigidity), tile_view(inv_mass), tile_view(gust_load)
     )
     wide = far - 1
-    low, high = exchanged(
+    still_inner, still_outer = exchanged(
         jnp.concatenate([stiff[:wide], pull[:near], push[:near]]),
         jnp.concatenate([stiff[rows - wide:], pull[rows - near:], push[rows - near:]]),
         odd,
     )
-    stiff = jnp.concatenate([low[:wide], stiff, high[:wide]])
-    pull = jnp.concatenate([low[wide:wide + near], pull, high[wide:wide + near]])
-    push = jnp.concatenate([low[wide + near:], push, high[wide + near:]])
 
     first = time_slot == 0
     edge = jnp.where(first, edge_own, edge_in)
     mid = jnp.where(first, mid_own, mid_in)
-    low, high = exchanged(edge[:side], edge[side:2 * side], odd)
-    inside = rows - 2 * far
-    position = jnp.concatenate(
-        [low[:far], edge[:far], mid[:inside], edge[side:side + far], high[:far]]
-    )
-    velocity = jnp.concatenate(
-        [low[far:], edge[far:side], mid[inside:], edge[side + far:2 * side], high[far:]]
-    )
+    inner, outer = exchanged(edge[:side], edge[side:2 * side], odd)
     gusts = jnp.stack([edge[2 * side], edge_own[2 * side]])
-
-    out = chain_call(
-        time_slot.reshape(1), position, velocity, stiff, pull, push, gusts, rows, far
+    slot = time_slot.reshape(1)
+    pos, vel = inner_call(slot, edge, mid, stiff, pull, push, gusts, rows, far)
+
+    low = jnp.where(odd, still_inner, still_outer)
+    high = jnp.where(odd, still_outer, still_inner)
+
+    def spread(low_rows, own_rows, high_rows):
+        margin = far + 2 - low_rows.shape[0]
+        block = jnp.concatenate([low_rows, own_rows, high_rows])
+        return jnp.pad(block, ((margin, margin), (0, 0), (0, 0)))
+
+    stiff = spread(low[:wide], stiff, high[:wide])
+    pull = spread(low[wide:wide + near], pull, high[wide:wide + near])
+    push = spread(low[wide + near:], push, high[wide + near:])
+    parity = odd.astype(jnp.int32).reshape(1)
+    out = outer_call(
+        slot, parity, inner, outer, stiff, pull, push, gusts, pos, vel, rows, far
     )
     return from_tile_view(out, start_state.shape)
 
@@ -506,7 +599,7 @@
 
 def chosen_device(start_state, rigidity, inv_mass, gust_load, kl_coeff, gust_history):
     rows, cols = rigidity.shape
-    fits = cols == SUBLANES * LANES and rows % SUBLANES == 0 and rows > 4 * (2 * FINE + 1)
+    fits = cols == SUBLANES * LANES and rows % SUBLANES == 0 and rows >= 2 * UNROLL
     two_slices = lax.axis_size("tm") == 2 and ITERS == 2 and start_state.shape[0] == 1
     device = layered_device if fits and two_slices else per_device
     return device(start_state, rigidity, inv_mass, gust_load, kl_coeff, gust_history)

time: 35.4 us -> 31.1 us (0.88); the launches traced: 34.8 us -> 30.9 us
  waiting for transfers between devices: 10.8 us -> 8.6 us
  local copies, waits for them, and re-layouts: 1.77 us -> 0.07 us
    ppermute x2, waiting for transfers between devices: 4.52 us -> 2.34 us  [exchanged(): lax.ppermute(jnp.where(odd, high_rows, low_rows), 'space', swap_pairs(cou...]
    unnamed x16 -> x0, local copies, waits for them, and re-layouts: 1.68 us -> none
    pallas_call x1, Pallas kernels: 1.01 us -> 2.12 us  [field_call(): pl.pallas_call(field_kernel, out_shape=(plane(rows),) * 3, in_specs=in_sm...]
    pallas_call x1 -> x2, Pallas kernels: 8.41 us -> 7.47 us  [the longest x1 3.74 us: outer_call(): pl.pallas_call(functools.partial(outer_kernel, rows=rows, far=far), out_s...]
  transfers between devices with their start and end apart: 6 -> 6, of which waited for: 4 -> 3; matrix products, arithmetic and copies ran while one was open for 1% -> 1% of each run, Pallas kernels for 0% -> 12%
where the time goes in v4:
time: 31.1 us; the launch traced here: 30.9 us
  Pallas kernels  10.7 us (34%)
  starting transfers between devices  10.7 us (34%)
  waiting for transfers between devices  8.6 us (28%)
  other arithmetic  0.54 us (2%)
    ppermute x2, starting transfers between devices, exchanged(): lax.ppermute(jnp.where(odd, high_rows, low_rows), 'space', swap_pairs(cou...  7.31 us
    ppermute x2, waiting for transfers between devices, passed_along(): return lax.ppermute(block, axis, route)  6.25 us
    pallas_call x1, Pallas kernels, outer_call(): pl.pallas_call(functools.partial(outer_kernel, rows=rows, far=far), out_s...  3.74 us
    pallas_call x1, Pallas kernels, inner_call(): pl.pallas_call(functools.partial(inner_kernel, rows=rows, far=far), out_s...  3.73 us
    ppermute x2, starting transfers between devices, passed_along(): return lax.ppermute(block, axis, route)  2.58 us
    ppermute x2, waiting for transfers between devices, exchanged(): lax.ppermute(jnp.where(odd, high_rows, low_rows), 'space', swap_pairs(cou...  2.34 us
    pallas_call x1, Pallas kernels, field_call(): pl.pallas_call(field_kernel, out_shape=(plane(rows),) * 3, in_specs=in_sm...  2.12 us
    pallas_call x1, Pallas kernels, two_slice_device(): pl.pallas_call(functools.partial(pack_kernel, rows=rows, far=far, near=ne...  1.12 us
  transfers between devices with their start and end apart: 6, of which 3 were waited for; matrix products, arithmetic and copies ran while one was open for 1% of the time, Pallas kernels for 12%

profile of v4, /device:TPU:7, one launch (start us, length us, event | category | flops | bytes accessed | tf_op | source)
XLA Modules:
  0.0 30.9 jit_solution(663893296442500193)
XLA Ops:
  0.0 0.1 multiply_cosine_fusion.1.across_ref
  0.2 0.1 multiply_cosine_fusion.along_ref
  0.3 1.1 %pack.1 = (f32[69,8,128]{2,1,0:T(8,128)S(1)}, f32[60,8,128]{2,1,0:T(8,128)S(1)}) custom-call(f32[4]{0:T(128)} %gust_hbm.1, f32[1024,128]{1,0:T(8,128)} %bitcast.27), custom_call_target="tpu_custom_call" | custom-call | tf_op jit(solution)/shard_map/pack/pallas_call | solution.py:539
  1.4 2.1 %field.1 = (f32[64,8,128]{2,1,0:T(8,128)S(1)}, f32[64,8,128]{2,1,0:T(8,128)S(1)}, f32[64,8,128]{2,1,0:T(8,128)S(1)}) custom-call(f32[4,64]{1,0:T(4,128)S(1)} %multiply_cosine_fusion.1.across_ref, f32[4,8,128]{2,1,0:T(8,128)S(1)} %multiply_cosine_fusion.along_ref, f32[4,4]{1,0:T(4,128)} %kl_hbm.1, f32[512,128]{1,0:T(8,128)} %bitcast.28, f32[512,128]{1,0:T(8,128)} %bitcast.29, ...), custom_call_target="tpu_custom_call" | custom-call | tf_op jit(solution)/shard_map/field/pallas_call | solution.py:473
  3.6 0.7 %collective-permute-start.3 = (f32[49,8,128]{2,1,0:T(8,128)S(1)}, f32[49,8,128]{2,1,0:T(8,128)S(1)}, u32[]{:S(2)}, u32[]{:S(2)}) collective-permute-start(f32[49,8,128]{2,1,0:T(8,128)S(1)} %get-tuple-element.31), channel_id=1, source_target_pairs={{0,1},{2,3},{4,5},{6,7},{8,9},{10,11},{12,13},{14,15},{1,0},{3,2},... | collective-permute-start | bytes 602120 | tf_op jit(solution)/shard_map/ppermute | solution.py:450
  4.4 3.0 %collective-permute-start.4 = (f32[49,8,128]{2,1,0:T(8,128)S(1)}, f32[49,8,128]{2,1,0:T(8,128)S(1)}, u32[]{:S(2)}, u32[]{:S(2)}) collective-permute-start(f32[49,8,128]{2,1,0:T(8,128)S(1)} %get-tuple-element.32), channel_id=1, source_target_pairs={{1,2},{3,4},{5,6},{7,8},{9,10},{11,12},{13,14},{2,1},{4,3},{6,5},{... | collective-permute-start | bytes 602120 | tf_op jit(solution)/shard_map/ppermute | solution.py:451
  7.4 1.3 %collective-permute-start = (f32[69,8,128]{2,1,0:T(8,128)S(1)}, f32[69,8,128]{2,1,0:T(8,128)S(1)}, u32[]{:S(2)}, u32[]{:S(2)}) collective-permute-start(f32[69,8,128]{2,1,0:T(8,128)S(1)} %get-tuple-element.18), channel_id=1, source_target_pairs={{0,16},{1,17},{2,18},{3,19},{4,20},{5,21},{6,22},{7,23},{8,24},{9,... | collective-permute-start | bytes 847880 | tf_op jit(solution)/shard_map/ppermute | solution.py:38
  8.7 1.3 %collective-permute-start.5 = (f32[60,8,128]{2,1,0:T(8,128)S(1)}, f32[60,8,128]{2,1,0:T(8,128)S(1)}, u32[]{:S(2)}, u32[]{:S(2)}) collective-permute-start(f32[60,8,128]{2,1,0:T(8,128)S(1)} %get-tuple-element.25), channel_id=1, source_target_pairs={{0,16},{1,17},{2,18},{3,19},{4,20},{5,21},{6,22},{7,23},{8,24},{9,... | collective-permute-start | bytes 737288 | tf_op jit(solution)/shard_map/ppermute | solution.py:38
  10.1 0.0 collective-permute-done.3
  10.1 2.3 %collective-permute-done.4 = f32[49,8,128]{2,1,0:T(8,128)S(1)} collective-permute-done((f32[49,8,128]{2,1,0:T(8,128)S(1)}, f32[49,8,128]{2,1,0:T(8,128)S(1)}, u32[]{:S(2)}, u32[]{:S(2)}) %collective-permute-start.4) | collective-permute-done | bytes 200736 | tf_op jit(solution)/shard_map/ppermute | solution.py:451
  12.4 0.1 broadcast_select_fusion.3
  12.6 0.1 select_maximum_fusion
  12.6 5.5 %collective-permute-done = f32[69,8,128]{2,1,0:T(8,128)S(1)} collective-permute-done((f32[69,8,128]{2,1,0:T(8,128)S(1)}, f32[69,8,128]{2,1,0:T(8,128)S(1)}, u32[]{:S(2)}, u32[]{:S(2)}) %collective-permute-start) | collective-permute-done | bytes 282656 | tf_op jit(solution)/shard_map/ppermute | solution.py:38
  18.2 4.3 %collective-permute-start.2 = (f32[34,8,128]{2,1,0:T(8,128)S(1)}, f32[34,8,128]{2,1,0:T(8,128)S(1)}, u32[]{:S(2)}, u32[]{:S(2)}) collective-permute-start(f32[34,8,128]{2,1,0:T(8,128)S(1)} %get-tuple-element.33), channel_id=1, source_target_pairs={{1,2},{3,4},{5,6},{7,8},{9,10},{11,12},{13,14},{2,1},{4,3},{6,5},{... | collective-permute-start | bytes 417800 | tf_op jit(solution)/shard_map/ppermute | solution.py:451
  22.4 0.1 collective-permute-start.1
  22.5 0.8 %collective-permute-done.5 = f32[60,8,128]{2,1,0:T(8,128)S(1)} collective-permute-done((f32[60,8,128]{2,1,0:T(8,128)S(1)}, f32[60,8,128]{2,1,0:T(8,128)S(1)}, u32[]{:S(2)}, u32[]{:S(2)}) %collective-permute-start.5) | collective-permute-done | bytes 245792 | tf_op jit(solution)/shard_map/ppermute | solution.py:38
  23.4 3.7 %inner.1 = (f32[10,104,8,128]{3,2,1,0:T(8,128)S(1)}, f32[10,104,8,128]{3,2,1,0:T(8,128)S(1)}) custom-call(s32[1]{0:T(128)} %bitcast.slot_ref, f32[69,8,128]{2,1,0:T(8,128)S(1)} %broadcast_select_fusion.edge_ref, f32[60,8,128]{2,1,0:T(8,128)S(1)} %broadcast_select_fusion.1.mid_ref, f32[64,8,128]{2,1,0:T(8,128)S(1)} %get-tuple-element.22.stiff_ref, ...), custom_call_target="tpu_custom_call" | custom-call | tf_op jit(solution)/shard_map/inner/pallas_call | solution.py:503
  27.1 0.0 collective-permute-done.2.outer_halo
  27.1 0.0 collective-permute-done.1.inner_halo
  27.1 3.7 %outer.1 = (f32[10,104,8,128]{3,2,1,0:T(8,128)S(1)}, f32[10,104,8,128]{3,2,1,0:T(8,128)S(1)}, f32[1024,128]{1,0:T(8,128)}) custom-call(s32[1]{0:T(128)} %bitcast.slot_ref, s32[1]{0:T(128)} %bitcast.1.odd_ref, f32[34,8,128]{2,1,0:T(8,128)S(1)} %collective-permute-done.1.inner_halo, ...), custom_call_target="tpu_custom_call", output_to_operand_aliasing={{0}: (8, {}), {1}: (9, {})} | custom-call | tf_op jit(solution)/shard_map/outer/pallas_call | solution.py:517
  (18 shorter events, 0.3 us)
Async XLA Ops:
  3.6 6.4 %collective-permute-start.3 = (f32[49,8,128]{2,1,0:T(8,128)S(1)}, f32[49,8,128]{2,1,0:T(8,128)S(1)}, u32[]{:S(2)}, u32[]{:S(2)}) collective-permute-start(f32[49,8,128]{2,1,0:T(8,128)S(1)} %get-tuple-element.31), channel_id=1, source_target_pairs={{0,1},{2,3},{4,5},{6,7},{8,9},{10,11},{12,13},{14,15},{1,0},{3,2},... | collective-permute-start | bytes 602120 | tf_op jit(solution)/shard_map/ppermute | solution.py:450
  4.4 8.0 %collective-permute-start.4 = (f32[49,8,128]{2,1,0:T(8,128)S(1)}, f32[49,8,128]{2,1,0:T(8,128)S(1)}, u32[]{:S(2)}, u32[]{:S(2)}) collective-permute-start(f32[49,8,128]{2,1,0:T(8,128)S(1)} %get-tuple-element.32), channel_id=1, source_target_pairs={{1,2},{3,4},{5,6},{7,8},{9,10},{11,12},{13,14},{2,1},{4,3},{6,5},{... | collective-permute-start | bytes 602120 | tf_op jit(solution)/shard_map/ppermute | solution.py:451
  7.4 10.7 %collective-permute-start = (f32[69,8,128]{2,1,0:T(8,128)S(1)}, f32[69,8,128]{2,1,0:T(8,128)S(1)}, u32[]{:S(2)}, u32[]{:S(2)}) collective-permute-start(f32[69,8,128]{2,1,0:T(8,128)S(1)} %get-tuple-element.18), channel_id=1, source_target_pairs={{0,16},{1,17},{2,18},{3,19},{4,20},{5,21},{6,22},{7,23},{8,24},{9,... | collective-permute-start | bytes 847880 | tf_op jit(solution)/shard_map/ppermute | solution.py:38
  8.7 14.6 %collective-permute-start.5 = (f32[60,8,128]{2,1,0:T(8,128)S(1)}, f32[60,8,128]{2,1,0:T(8,128)S(1)}, u32[]{:S(2)}, u32[]{:S(2)}) collective-permute-start(f32[60,8,128]{2,1,0:T(8,128)S(1)} %get-tuple-element.25), channel_id=1, source_target_pairs={{0,16},{1,17},{2,18},{3,19},{4,20},{5,21},{6,22},{7,23},{8,24},{9,... | collective-permute-start | bytes 737288 | tf_op jit(solution)/shard_map/ppermute | solution.py:38
  18.2 8.9 %collective-permute-start.2 = (f32[34,8,128]{2,1,0:T(8,128)S(1)}, f32[34,8,128]{2,1,0:T(8,128)S(1)}, u32[]{:S(2)}, u32[]{:S(2)}) collective-permute-start(f32[34,8,128]{2,1,0:T(8,128)S(1)} %get-tuple-element.33), channel_id=1, source_target_pairs={{1,2},{3,4},{5,6},{7,8},{9,10},{11,12},{13,14},{2,1},{4,3},{6,5},{... | collective-permute-start | bytes 417800 | tf_op jit(solution)/shard_map/ppermute | solution.py:451
  22.4 4.7 %collective-permute-start.1 = (f32[34,8,128]{2,1,0:T(8,128)S(1)}, f32[34,8,128]{2,1,0:T(8,128)S(1)}, u32[]{:S(2)}, u32[]{:S(2)}) collective-permute-start(f32[34,8,128]{2,1,0:T(8,128)S(1)} %get-tuple-element.34), channel_id=1, source_target_pairs={{0,1},{2,3},{4,5},{6,7},{8,9},{10,11},{12,13},{14,15},{1,0},{3,2},... | collective-permute-start | bytes 417800 | tf_op jit(solution)/shard_map/ppermute | solution.py:450

commit v5 on v4

--- a/solution.py
+++ b/solution.py
@@ -171,7 +171,7 @@
 DECAY = 1.0 - HALF_STEP * DAMPING
 COARSE_DECAY = 1.0 - COARSE_SPAN * DAMPING
 KICK = TIME_STEP * HALF_STEP
-UNROLL = 32
+UNROLL = 60
 
 
 def tile_view(block):
@@ -191,8 +191,23 @@
     return view_ref[pl.ds(start + row, SUBLANES, stride=SUBLANES), :]
 
 
-def pack_kernel(
-    gust_hbm, view_hbm, edge_ref, mid_ref, view_ref, gust_ref, sems, *, rows, far, near
+def gusts_of(gust_ref):
+    sub = lax.broadcasted_iota(jnp.int32, (SUBLANES, LANES), 0)
+    gusts = jnp.zeros((SUBLANES, LANES), jnp.float32)
+    for step_index in range(FINE):
+        gusts = jnp.where(sub == step_index, gust_ref[step_index], gusts)
+    return gusts
+
+
+def pack_kernel(slot_ref, odd_ref, *refs, rows, far):
+    @pl.when(slot_ref[0] == 0)
+    def _():
+        pack_rows(odd_ref, *refs, rows=rows, far=far)
+
+
+def pack_rows(
+    odd_ref, gust_hbm, view_hbm, first_ref, second_ref, mid_ref, view_ref, gust_ref, sems,
+    *, rows, far
 ):
     gust_copy = pltpu.make_async_copy(gust_hbm, gust_ref, sems.at[2])
     half = rows * SUBLANES
@@ -204,35 +219,45 @@
         )
         copies[part].start()
     gust_copy.start()
-    side = far + near
-    for part, width, at in ((0, far, 0), (1, near, far)):
+    near = far - 2
+    parts = ((0, far, 0), (1, near, far))
+
+    def state_row(part, row):
+        return row_at(view_ref, (part * rows + row) // SUBLANES, row % SUBLANES)
+
+    def edges(low_ref, high_ref):
+        for part, width, at in parts:
+            for i in range(width):
+                low_ref[at + i] = state_row(part, i)
+                high_ref[at + i] = state_row(part, rows - width + i)
+
+    for part, width, at in parts:
         copies[part].wait()
-        for row in range(rows):
-            group = (part * rows + row) // SUBLANES
-            value = row_at(view_ref, group, row % SUBLANES)
-            if row < width:
-                edge_ref[at + row] = value
-            elif row >= rows - width:
-                edge_ref[side + at + row - (rows - width)] = value
-            else:
-                mid_ref[part * (rows - 2 * far) + row - width] = value
+        for row in range(width, rows - width):
+            mid_ref[part * (rows - 2 * far) + row - width] = state_row(part, row)
+
+    @pl.when(odd_ref[0] == 0)
+    def _():
+        edges(first_ref, second_ref)
+
+    @pl.when(odd_ref[0] != 0)
+    def _():
+        edges(second_ref, first_ref)
+
     gust_copy.wait()
-    sub = lax.broadcasted_iota(jnp.int32, (SUBLANES, LANES), 0)
-    gusts = jnp.zeros((SUBLANES, LANES), jnp.float32)
-    for step_index in range(FINE):
-        gusts = jnp.where(sub == step_index, gust_ref[step_index], gusts)
-    edge_ref[2 * side] = gusts
+    first_ref[far + near] = gusts_of(gust_ref)
 
 
 def field_kernel(
-    across_ref, along_ref, kl_hbm, rigid_hbm, mass_hbm, load_hbm, stiff_ref, pull_ref, push_ref,
-    kl_ref, rigid_ref, mass_ref, load_ref, sems
+    across_ref, along_ref, kl_hbm, gust_hbm, rigid_hbm, mass_hbm, load_hbm, stiff_ref, pull_ref,
+    push_ref, gust_out, kl_ref, gust_ref, rigid_ref, mass_ref, load_ref, sems
 ):
     copies = [
         pltpu.make_async_copy(source, target, sems.at[at])
         for at, (source, target) in enumerate(
             (
                 (kl_hbm, kl_ref),
+                (gust_hbm, gust_ref),
                 (rigid_hbm, rigid_ref),
                 (mass_hbm, mass_ref),
                 (load_hbm, load_ref),
@@ -241,8 +266,9 @@
     ]
     for copy in copies:
         copy.start()
-    for copy in copies:
+    for copy in copies[:2]:
         copy.wait()
+    gust_out[...] = gusts_of(gust_ref)
     rows = stiff_ref.shape[0]
     mixed = []
     for order in range(KL):
@@ -251,14 +277,24 @@
             total = total + kl_ref[order, other] * along_ref[other]
         mixed.append(total)
 
-    def group_rows(group, carry):
+    def factor_rows(group, carry):
         for row in range(SUBLANES):
             at = group * SUBLANES + row
             field = across_ref[0, at] * mixed[0]
             for order in range(1, KL):
                 field = field + across_ref[order, at] * mixed[order]
+            stiff_ref[at] = jnp.exp(0.5 * jnp.tanh(field))
+        return carry
+
+    lax.fori_loop(0, rows // SUBLANES, factor_rows, 0)
+    for copy in copies[2:]:
+        copy.wait()
+
+    def group_rows(group, carry):
+        for row in range(SUBLANES):
+            at = group * SUBLANES + row
             mass = row_at(mass_ref, group, row)
-            stiff_ref[at] = row_at(rigid_ref, group, row) * jnp.exp(0.5 * jnp.tanh(field))
+            stiff_ref[at] = row_at(rigid_ref, group, row) * stiff_ref[at]
             pull_ref[at] = (KICK * (1.0 + DECAY) * STIFF_SCALE) * mass
             push_ref[at] = KICK * (mass * row_at(load_ref, group, row))
         return carry
@@ -271,10 +307,10 @@
     sub = lax.broadcasted_iota(jnp.int32, (SUBLANES, LANES), 0)
     last_lane = lane == LANES - 1
     first_lane = lane == 0
-    below = jnp.where(last_lane, pltpu.roll(row, 1, 0), row)
-    above = jnp.where(first_lane, pltpu.roll(row, SUBLANES - 1, 0), row)
-    below = jnp.where(last_lane & (sub == 0), 0.0, below)
-    above = jnp.where(first_lane & (sub == SUBLANES - 1), 0.0, above)
+    ends = (last_lane & (sub == SUBLANES - 1)) | (first_lane & (sub == 0))
+    within = jnp.where(ends, 0.0, row)
+    below = jnp.where(last_lane, pltpu.roll(within, 1, 0), row)
+    above = jnp.where(first_lane, pltpu.roll(within, SUBLANES - 1, 0), row)
     return pltpu.roll(below, 1, 1) + pltpu.roll(above, LANES - 1, 1)
 
 
@@ -313,25 +349,30 @@
         coef[FINE, 2] = splat(HALF_PULL / TIME_STEP)
 
 
-def advance_rows(sweep, start, count, offset, pos, vel, coef, stiff_ref, pull_ref, push_ref):
-    here = [pos[sweep, start - 2 + i] for i in range(count + 4)]
-    sides = [beside(here[i]) for i in range(1, count + 3)]
+def advance_rows(sweep, starts, count, offset, pos, vel, coef, stiff_ref, pull_ref, push_ref):
+    here = [[pos[sweep, start - 2 + i] for i in range(count + 4)] for start in starts]
+    sides = [[beside(rows[i]) for i in range(1, count + 3)] for rows in here]
     weighted = [
-        stiff_ref[start - 1 + i - offset]
-        * (here[i] + here[i + 2] + sides[i] - 4.0 * here[i + 1])
-        for i in range(count + 2)
+        [
+            stiff_ref[start - 1 + i - offset]
+            * (rows[i] + rows[i + 2] + side[i] - 4.0 * rows[i + 1])
+            for i in range(count + 2)
+        ]
+        for start, rows, side in zip(starts, here, sides)
     ]
+    weighted_sides = [[beside(row) for row in rows[1:-1]] for rows in weighted]
     alpha, push_by, pull_by = (coef[sweep, i] for i in range(3))
     moved = []
-    for i in range(count):
-        row = start + i
-        bent = weighted[i] + weighted[i + 2] + beside(weighted[i + 1]) - 4.0 * weighted[i + 1]
-        shift = (
-            alpha * vel[sweep, row]
-            + push_by * push_ref[row - offset]
-            - pull_by * (pull_ref[row - offset] * bent)
-        )
-        moved.append((row, here[i + 2] + shift, shift))
+    for start, rows, heavy, side in zip(starts, here, weighted, weighted_sides):
+        for i in range(count):
+            row = start + i
+            bent = heavy[i] + heavy[i + 2] + side[i] - 4.0 * heavy[i + 1]
+            shift = (
+                alpha * vel[sweep, row]
+                + push_by * push_ref[row - offset]
+                - pull_by * (pull_ref[row - offset] * bent)
+            )
+            moved.append((row, rows[i + 2] + shift, shift))
     return moved
 
 
@@ -358,21 +399,21 @@
         for i in range(rows - 2 * width):
             plane_ref[0, top + width + i] = mid_ref[first + i]
 
-    def sweep_all(sweep, carry):
-        first = 2 * sweep + 2
-        end = rows - first
-
-        def chunk(index, carry):
-            start = jnp.minimum(first + index * UNROLL, end - UNROLL) + top
+    def sweep_with(count):
+        def sweep_all(sweep, carry):
+            start = top + (rows - count) // 2
             moved = advance_rows(
-                sweep, start, UNROLL, top, pos, vel, coef, stiff_ref, pull_ref, push_ref
+                sweep, (start,), count, top, pos, vel, coef, stiff_ref, pull_ref, push_ref
             )
             keep_rows(sweep, moved, pos, vel)
             return carry
 
-        return lax.fori_loop(0, (end - first + UNROLL - 1) // UNROLL, chunk, carry)
-
-    lax.fori_loop(0, jnp.where(slot == 0, FINE + 1, 2 * FINE + 1), sweep_all, 0)
+        return sweep_all
+
+    early = 4
+    sweeps = jnp.where(slot == 0, FINE + 1, 2 * FINE + 1)
+    lax.fori_loop(0, early, sweep_with(rows - 4), 0)
+    lax.fori_loop(early, sweeps, sweep_with(rows - 4 - 4 * early), 0)
 
 
 def outer_kernel(
@@ -402,11 +443,10 @@
         fill_halo(inner_halo, outer_halo)
 
     def sweep_all(sweep, carry):
-        moved = []
-        for start in (top - near + 2 * sweep, top + rows - 2 - 2 * sweep):
-            moved += advance_rows(
-                sweep, start, far, 0, pos, vel, coef, stiff_ref, pull_ref, push_ref
-            )
+        starts = (top - near + 2 * sweep, top + rows - 2 - 2 * sweep)
+        moved = advance_rows(
+            sweep, starts, far, 0, pos, vel, coef, stiff_ref, pull_ref, push_ref
+        )
         keep_rows(sweep, moved, pos, vel)
         return carry
 
@@ -445,11 +485,12 @@
     return pairs + [(target, source) for source, target in pairs]
 
 
-def exchanged(low_rows, high_rows, odd):
-    count = lax.axis_size("space")
-    inner = lax.ppermute(jnp.where(odd, low_rows, high_rows), "space", swap_pairs(count, 0))
-    outer = lax.ppermute(jnp.where(odd, high_rows, low_rows), "space", swap_pairs(count, 1))
-    return inner, outer
+def sent(block, pairs, within=None):
+    if within is not None:
+        base = within * lax.axis_size("space")
+        pairs = [(base + source, base + target) for source, target in pairs]
+    axes = "space" if within is None else ("tm", "space")
+    return lax.ppermute(block, axes, pairs)
 
 
 def in_vmem(count):
@@ -468,22 +509,26 @@
     return jax.ShapeDtypeStruct((count, SUBLANES, LANES), jnp.float32)
 
 
-def field_call(across, along, kl_coeff, rigidity, inv_mass, gust_load):
+def field_call(across, along, kl_coeff, gust_history, rigidity, inv_mass, gust_load):
     rows = rigidity.shape[0] // SUBLANES
     return pl.pallas_call(
         field_kernel,
-        out_shape=(plane(rows),) * 3,
-        in_specs=in_smem(1) + in_vmem(1) + [pl.BlockSpec(memory_space=pltpu.HBM)] * 4,
-        out_specs=tuple(in_vmem(3)),
-        scratch_shapes=[pltpu.SMEM((KL, KL), jnp.float32)]
+        out_shape=(plane(rows),) * 3 + (jax.ShapeDtypeStruct((SUBLANES, LANES), jnp.float32),),
+        in_specs=in_smem(1) + in_vmem(1) + [pl.BlockSpec(memory_space=pltpu.HBM)] * 5,
+        out_specs=tuple(in_vmem(4)),
+        scratch_shapes=[
+            pltpu.SMEM((KL, KL), jnp.float32),
+            pltpu.SMEM((FINE,), jnp.float32),
+        ]
         + [pltpu.VMEM(rigidity.shape, jnp.float32)] * 3
-        + [pltpu.SemaphoreType.DMA((4,))],
+        + [pltpu.SemaphoreType.DMA((5,))],
         compiler_params=pltpu.CompilerParams(vmem_limit_bytes=16 * 2**20),
         name="field",
     )(
         across,
         along,
         in_hbm(kl_coeff),
+        in_hbm(gust_history),
         in_hbm(rigidity),
         in_hbm(inv_mass),
         in_hbm(gust_load),
@@ -533,14 +578,17 @@
     side = far + near
     time_slot = lax.axis_index("tm")
     space_slot = lax.axis_index("space")
+    space_count = lax.axis_size("space")
     odd = space_slot % 2 == 1
     small = pltpu.CompilerParams(vmem_limit_bytes=16 * 2**20)
 
-    edge_own, mid_own = pl.pallas_call(
-        functools.partial(pack_kernel, rows=rows, far=far, near=near),
-        out_shape=(plane(2 * side + 1), plane(2 * rows - 2 * side)),
-        in_specs=[pl.BlockSpec(memory_space=pltpu.HBM)] * 2,
-        out_specs=tuple(in_vmem(2)),
+    slot = time_slot.reshape(1)
+    parity = odd.astype(jnp.int32).reshape(1)
+    first_own, second_own, mid_own = pl.pallas_call(
+        functools.partial(pack_kernel, rows=rows, far=far),
+        out_shape=(plane(side + 1), plane(side), plane(2 * rows - 2 * side)),
+        in_specs=in_smem(2) + [pl.BlockSpec(memory_space=pltpu.HBM)] * 2,
+        out_specs=tuple(in_vmem(3)),
         scratch_shapes=[
             pltpu.VMEM((2 * rows * SUBLANES, LANES), jnp.float32),
             pltpu.SMEM((FINE,), jnp.float32),
@@ -548,33 +596,60 @@
         ],
         compiler_params=small,
         name="pack",
-    )(in_hbm(gust_history), in_hbm(tile_view(start_state)))
-    edge_in = passed_along(edge_own, "tm", 1)
+    )(slot, parity, in_hbm(gust_history), in_hbm(tile_view(start_state)))
+    first_in = passed_along(first_own, "tm", 1)
+    few = 2 * (FINE + 1)
+    away = far - few
+    early_rows = jnp.where(
+        odd,
+        jnp.concatenate([first_own[away:far], first_own[far + away:side]]),
+        jnp.concatenate([first_own[:few], first_own[far:side - away]]),
+    )
+    early = sent(early_rows, swap_pairs(space_count, 1), 0)
+    second_in = passed_along(second_own, "tm", 1)
     mid_in = passed_along(mid_own, "tm", 1)
-    edge_own, rigidity, inv_mass, gust_load = lax.optimization_barrier(
-        (edge_own, rigidity, inv_mass, gust_load)
+    first_own, rigidity, inv_mass, gust_load = lax.optimization_barrier(
+        (first_own, rigidity, inv_mass, gust_load)
     )
 
     across = mode_table(space_slot * rows + jnp.arange(rows), rows * lax.axis_size("space"))
     along = mode_table(jnp.arange(cols), cols).reshape(KL, SUBLANES, LANES)
-    stiff, pull, push = field_call(
-        across, along, kl_coeff, tile_view(rigidity), tile_view(inv_mass), tile_view(gust_load)
+    stiff, pull, push, own_gusts = field_call(
+        across,
+        along,
+        kl_coeff,
+        gust_history,
+        tile_view(rigidity),
+        tile_view(inv_mass),
+        tile_view(gust_load),
     )
     wide = far - 1
-    still_inner, still_outer = exchanged(
-        jnp.concatenate([stiff[:wide], pull[:near], push[:near]]),
-        jnp.concatenate([stiff[rows - wide:], pull[rows - near:], push[rows - near:]]),
-        odd,
-    )
-
-    first = time_slot == 0
-    edge = jnp.where(first, edge_own, edge_in)
-    mid = jnp.where(first, mid_own, mid_in)
-    inner, outer = exchanged(edge[:side], edge[side:2 * side], odd)
-    gusts = jnp.stack([edge[2 * side], edge_own[2 * side]])
-    slot = time_slot.reshape(1)
+    still_low = jnp.concatenate([stiff[:wide], pull[:near], push[:near]])
+    still_high = jnp.concatenate(
+        [stiff[rows - wide:], pull[rows - near:], push[rows - near:]]
+    )
+    still_outer = sent(jnp.where(odd, still_high, still_low), swap_pairs(space_count, 1))
+    still_inner = sent(jnp.where(odd, still_low, still_high), swap_pairs(space_count, 0))
+
+    own = time_slot == 0
+    first_edge = jnp.where(own, first_own, first_in)
+    mid = jnp.where(own, mid_own, mid_in)
+    outer_late = sent(first_in, swap_pairs(space_count, 1), 1)
+    second_edge = jnp.where(own, second_own, second_in)
+    edge = jnp.concatenate(
+        [
+            jnp.where(odd, second_edge, first_edge[:side]),
+            jnp.where(odd, first_edge[:side], second_edge),
+        ]
+    )
+    inner = sent(second_edge, swap_pairs(space_count, 0))
+    gusts = jnp.stack([first_edge[side], own_gusts])
     pos, vel = inner_call(slot, edge, mid, stiff, pull, push, gusts, rows, far)
 
+    blank = jnp.zeros((away, SUBLANES, LANES), jnp.float32)
+    of_even = jnp.concatenate([early[:few], blank, early[few:], blank])
+    of_odd = jnp.concatenate([blank, early[:few], blank, early[few:]])
+    outer = jnp.where(own, jnp.where(odd, of_even, of_odd), outer_late[:side])
     low = jnp.where(odd, still_inner, still_outer)
     high = jnp.where(odd, still_outer, still_inner)
 
@@ -586,7 +661,6 @@
     stiff = spread(low[:wide], stiff, high[:wide])
     pull = spread(low[wide:wide + near], pull, high[wide:wide + near])
     push = spread(low[wide + near:], push, high[wide + near:])
-    parity = odd.astype(jnp.int32).reshape(1)
     out = outer_call(
         slot, parity, inner, outer, stiff, pull, push, gusts, pos, vel, rows, far
     )
@@ -599,7 +673,7 @@
 
 def chosen_device(start_state, rigidity, inv_mass, gust_load, kl_coeff, gust_history):
     rows, cols = rigidity.shape
-    fits = cols == SUBLANES * LANES and rows % SUBLANES == 0 and rows >= 2 * UNROLL
+    fits = cols == SUBLANES * LANES and rows % SUBLANES == 0 and rows >= UNROLL + 4
     two_slices = lax.axis_size("tm") == 2 and ITERS == 2 and start_state.shape[0] == 1
     device = layered_device if fits and two_slices else per_device
     return device(start_state, rigidity, inv_mass, gust_load, kl_coeff, gust_history)

time: 31.1 us -> 26 us (0.84)
  the two profiles are of different devices: /device:TPU:7 before, /device:TPU:9 now
where the time goes in v5:
time: 26 us; the launch traced here: 25.8 us
  starting transfers between devices  12.9 us (50%)
  Pallas kernels  7.11 us (27%)
  waiting for transfers between devices  4.73 us (18%)
  other arithmetic  0.59 us (2%)
  between operations  0.34 us (1%)
    ppermute x5, starting transfers between devices, sent(): return lax.ppermute(block, axes, pairs)  8.31 us
    ppermute x5, waiting for transfers between devices, sent(): return lax.ppermute(block, axes, pairs)  4.72 us
    ppermute x3, starting transfers between devices, passed_along(): return lax.ppermute(block, axis, route)  4.6 us
    pallas_call x1, Pallas kernels, outer_call(): pl.pallas_call(functools.partial(outer_kernel, rows=rows, far=far), out_s...  2.35 us
    pallas_call x1, Pallas kernels, field_call(): pl.pallas_call(field_kernel, out_shape=(plane(rows),) * 3 + (jax.ShapeDty...  1.92 us
    pallas_call x1, Pallas kernels, inner_call(): pl.pallas_call(functools.partial(inner_kernel, rows=rows, far=far), out_s...  1.68 us
    pallas_call x1, Pallas kernels, two_slice_device(): pl.pallas_call(functools.partial(pack_kernel, rows=rows, far=far), out_sh...  1.15 us
  transfers between devices with their start and end apart: 8, of which 1 were waited for; matrix products, arithmetic and copies ran while one was open for 3% of the time, Pallas kernels for 14%

profile of v5, /device:TPU:9, one launch (start us, length us, event | category | flops | bytes accessed | tf_op | source)
XLA Modules:
  0.0 25.8 jit_solution(8560689209787964374)
XLA Ops:
  0.0 1.1 %pack.1 = (f32[35,8,128]{2,1,0:T(8,128)S(1)}, f32[34,8,128]{2,1,0:T(8,128)S(1)}, f32[60,8,128]{2,1,0:T(8,128)S(1)}) custom-call(s32[1]{0:T(128)} %bitcast.slot_ref, s32[1]{0:T(128)} %bitcast.1.odd_ref, f32[4]{0:T(128)} %gust_hbm.1, f32[1024,128]{1,0:T(8,128)} %bitcast.29), custom_call_target="tpu_custom_call" | custom-call | tf_op jit(solution)/shard_map/pack/pallas_call | solution.py:587
  1.2 2.0 %collective-permute-start.3 = (f32[35,8,128]{2,1,0:T(8,128)S(1)}, f32[35,8,128]{2,1,0:T(8,128)S(1)}, u32[]{:S(2)}, u32[]{:S(2)}) collective-permute-start(f32[35,8,128]{2,1,0:T(8,128)S(1)} %get-tuple-element.27), channel_id=1, source_target_pairs={{0,16},{1,17},{2,18},{3,19},{4,20},{5,21},{6,22},{7,23},{8,24},{9,... | collective-permute-start | bytes 430088 | tf_op jit(solution)/shard_map/ppermute | solution.py:38
  3.2 4.0 %collective-permute-start.2 = (f32[18,8,128]{2,1,0:T(8,128)S(1)}, f32[18,8,128]{2,1,0:T(8,128)S(1)}, u32[]{:S(2)}, u32[]{:S(2)}) collective-permute-start(f32[18,8,128]{2,1,0:T(8,128)S(1)} %maximum_select_fusion.1), channel_id=1, source_target_pairs={{1,2},{3,4},{5,6},{7,8},{9,10},{11,12},{13,14},{2,1},{4,3},{6,5},{... | collective-permute-start | bytes 221192 | tf_op jit(solution)/shard_map/ppermute | solution.py:493
  7.2 1.3 %collective-permute-start = (f32[34,8,128]{2,1,0:T(8,128)S(1)}, f32[34,8,128]{2,1,0:T(8,128)S(1)}, u32[]{:S(2)}, u32[]{:S(2)}) collective-permute-start(f32[34,8,128]{2,1,0:T(8,128)S(1)} %get-tuple-element.19), channel_id=1, source_target_pairs={{0,16},{1,17},{2,18},{3,19},{4,20},{5,21},{6,22},{7,23},{8,24},{9,... | collective-permute-start | bytes 417800 | tf_op jit(solution)/shard_map/ppermute | solution.py:38
  8.5 1.3 %collective-permute-start.7 = (f32[60,8,128]{2,1,0:T(8,128)S(1)}, f32[60,8,128]{2,1,0:T(8,128)S(1)}, u32[]{:S(2)}, u32[]{:S(2)}) collective-permute-start(f32[60,8,128]{2,1,0:T(8,128)S(1)} %get-tuple-element.29), channel_id=1, source_target_pairs={{0,16},{1,17},{2,18},{3,19},{4,20},{5,21},{6,22},{7,23},{8,24},{9,... | collective-permute-start | bytes 737288 | tf_op jit(solution)/shard_map/ppermute | solution.py:38
  9.9 0.1 multiply_cosine_fusion.1.across_ref
  10.0 0.1 multiply_cosine_fusion.along_ref
  10.1 1.9 %field.1 = (f32[64,8,128]{2,1,0:T(8,128)S(1)}, f32[64,8,128]{2,1,0:T(8,128)S(1)}, f32[64,8,128]{2,1,0:T(8,128)S(1)}, f32[8,128]{1,0:T(8,128)S(1)}) custom-call(f32[4,64]{1,0:T(4,128)S(1)} %multiply_cosine_fusion.1.across_ref, f32[4,8,128]{2,1,0:T(8,128)S(1)} %multiply_cosine_fusion.along_ref, f32[4,4]{1,0:T(4,128)} %kl_hbm.1, f32[4]{0:T(128)} %gust_hbm.1, ...), custom_call_target="tpu_custom_call" | custom-call | tf_op jit(solution)/shard_map/field/pallas_call | solution.py:514
  12.2 0.1 collective-permute-start.5
  12.2 0.0 collective-permute-done.2
  12.2 3.5 %collective-permute-start.6 = (f32[49,8,128]{2,1,0:T(8,128)S(1)}, f32[49,8,128]{2,1,0:T(8,128)S(1)}, u32[]{:S(2)}, u32[]{:S(2)}) collective-permute-start(f32[49,8,128]{2,1,0:T(8,128)S(1)} %get-tuple-element.38), channel_id=1, source_target_pairs={{1,2},{3,4},{5,6},{7,8},{9,10},{11,12},{13,14},{2,1},{4,3},{6,5},{... | collective-permute-start | bytes 602120 | tf_op jit(solution)/shard_map/ppermute | solution.py:493
  15.8 0.0 collective-permute-done.3
  15.8 0.0 collective-permute-done
  15.9 0.1 collective-permute-start.1
  16.0 0.7 %collective-permute-start.4 = (f32[35,8,128]{2,1,0:T(8,128)S(1)}, f32[35,8,128]{2,1,0:T(8,128)S(1)}, u32[]{:S(2)}, u32[]{:S(2)}) collective-permute-start(f32[35,8,128]{2,1,0:T(8,128)S(1)} %collective-permute-done.3), channel_id=1, source_target_pairs={{17,18},{19,20},{21,22},{23,24},{25,26},{27,28},{29,30},{18,17},{2... | collective-permute-start | bytes 430088 | tf_op jit(solution)/shard_map/ppermute | solution.py:493
  16.7 0.0 collective-permute-done.5
  16.7 4.7 %collective-permute-done.6 = f32[49,8,128]{2,1,0:T(8,128)S(1)} collective-permute-done((f32[49,8,128]{2,1,0:T(8,128)S(1)}, f32[49,8,128]{2,1,0:T(8,128)S(1)}, u32[]{:S(2)}, u32[]{:S(2)}) %collective-permute-start.6) | collective-permute-done | bytes 200736 | tf_op jit(solution)/shard_map/ppermute | solution.py:493
  21.6 0.1 select_maximum_fusion
  21.6 0.0 collective-permute-done.7
  21.7 1.7 %inner.1 = (f32[10,104,8,128]{3,2,1,0:T(8,128)S(1)}, f32[10,104,8,128]{3,2,1,0:T(8,128)S(1)}) custom-call(s32[1]{0:T(128)} %bitcast.slot_ref, f32[68,8,128]{2,1,0:T(8,128)S(1)} %pad_maximum_fusion.edge_ref, f32[60,8,128]{2,1,0:T(8,128)S(1)} %broadcast_select_fusion.mid_ref, f32[64,8,128]{2,1,0:T(8,128)S(1)} %get-tuple-element.24.stiff_ref, ...), custom_call_target="tpu_custom_call" | custom-call | tf_op jit(solution)/shard_map/inner/pallas_call | solution.py:548
  23.4 0.0 collective-permute-done.4
  23.4 0.0 collective-permute-done.1.inner_halo
  23.4 2.4 %outer.1 = (f32[10,104,8,128]{3,2,1,0:T(8,128)S(1)}, f32[10,104,8,128]{3,2,1,0:T(8,128)S(1)}, f32[1024,128]{1,0:T(8,128)}) custom-call(s32[1]{0:T(128)} %bitcast.slot_ref, s32[1]{0:T(128)} %bitcast.1.odd_ref, f32[34,8,128]{2,1,0:T(8,128)S(1)} %collective-permute-done.1.inner_halo, ...), custom_call_target="tpu_custom_call", output_to_operand_aliasing={{0}: (8, {}), {1}: (9, {})} | custom-call | tf_op jit(solution)/shard_map/outer/pallas_call | solution.py:562
  (27 shorter events, 0.4 us)
Async XLA Ops:
  1.2 14.6 %collective-permute-start.3 = (f32[35,8,128]{2,1,0:T(8,128)S(1)}, f32[35,8,128]{2,1,0:T(8,128)S(1)}, u32[]{:S(2)}, u32[]{:S(2)}) collective-permute-start(f32[35,8,128]{2,1,0:T(8,128)S(1)} %get-tuple-element.27), channel_id=1, source_target_pairs={{0,16},{1,17},{2,18},{3,19},{4,20},{5,21},{6,22},{7,23},{8,24},{9,... | collective-permute-start | bytes 430088 | tf_op jit(solution)/shard_map/ppermute | solution.py:38
  3.2 9.0 %collective-permute-start.2 = (f32[18,8,128]{2,1,0:T(8,128)S(1)}, f32[18,8,128]{2,1,0:T(8,128)S(1)}, u32[]{:S(2)}, u32[]{:S(2)}) collective-permute-start(f32[18,8,128]{2,1,0:T(8,128)S(1)} %maximum_select_fusion.1), channel_id=1, source_target_pairs={{1,2},{3,4},{5,6},{7,8},{9,10},{11,12},{13,14},{2,1},{4,3},{6,5},{... | collective-permute-start | bytes 221192 | tf_op jit(solution)/shard_map/ppermute | solution.py:493
  7.2 8.6 %collective-permute-start = (f32[34,8,128]{2,1,0:T(8,128)S(1)}, f32[34,8,128]{2,1,0:T(8,128)S(1)}, u32[]{:S(2)}, u32[]{:S(2)}) collective-permute-start(f32[34,8,128]{2,1,0:T(8,128)S(1)} %get-tuple-element.19), channel_id=1, source_target_pairs={{0,16},{1,17},{2,18},{3,19},{4,20},{5,21},{6,22},{7,23},{8,24},{9,... | collective-permute-start | bytes 417800 | tf_op jit(solution)/shard_map/ppermute | solution.py:38
  8.5 13.1 %collective-permute-start.7 = (f32[60,8,128]{2,1,0:T(8,128)S(1)}, f32[60,8,128]{2,1,0:T(8,128)S(1)}, u32[]{:S(2)}, u32[]{:S(2)}) collective-permute-start(f32[60,8,128]{2,1,0:T(8,128)S(1)} %get-tuple-element.29), channel_id=1, source_target_pairs={{0,16},{1,17},{2,18},{3,19},{4,20},{5,21},{6,22},{7,23},{8,24},{9,... | collective-permute-start | bytes 737288 | tf_op jit(solution)/shard_map/ppermute | solution.py:38
  12.2 4.6 %collective-permute-start.5 = (f32[49,8,128]{2,1,0:T(8,128)S(1)}, f32[49,8,128]{2,1,0:T(8,128)S(1)}, u32[]{:S(2)}, u32[]{:S(2)}) collective-permute-start(f32[49,8,128]{2,1,0:T(8,128)S(1)} %get-tuple-element.37), channel_id=1, source_target_pairs={{0,1},{2,3},{4,5},{6,7},{8,9},{10,11},{12,13},{14,15},{1,0},{3,2},... | collective-permute-start | bytes 602120 | tf_op jit(solution)/shard_map/ppermute | solution.py:493
  12.2 9.2 %collective-permute-start.6 = (f32[49,8,128]{2,1,0:T(8,128)S(1)}, f32[49,8,128]{2,1,0:T(8,128)S(1)}, u32[]{:S(2)}, u32[]{:S(2)}) collective-permute-start(f32[49,8,128]{2,1,0:T(8,128)S(1)} %get-tuple-element.38), channel_id=1, source_target_pairs={{1,2},{3,4},{5,6},{7,8},{9,10},{11,12},{13,14},{2,1},{4,3},{6,5},{... | collective-permute-start | bytes 602120 | tf_op jit(solution)/shard_map/ppermute | solution.py:493
  15.9 7.5 %collective-permute-start.1 = (f32[34,8,128]{2,1,0:T(8,128)S(1)}, f32[34,8,128]{2,1,0:T(8,128)S(1)}, u32[]{:S(2)}, u32[]{:S(2)}) collective-permute-start(f32[34,8,128]{2,1,0:T(8,128)S(1)} %get-tuple-element.34), channel_id=1, source_target_pairs={{0,1},{2,3},{4,5},{6,7},{8,9},{10,11},{12,13},{14,15},{1,0},{3,2},... | collective-permute-start | bytes 417800 | tf_op jit(solution)/shard_map/ppermute | solution.py:493
  16.0 7.4 %collective-permute-start.4 = (f32[35,8,128]{2,1,0:T(8,128)S(1)}, f32[35,8,128]{2,1,0:T(8,128)S(1)}, u32[]{:S(2)}, u32[]{:S(2)}) collective-permute-start(f32[35,8,128]{2,1,0:T(8,128)S(1)} %collective-permute-done.3), channel_id=1, source_target_pairs={{17,18},{19,20},{21,22},{23,24},{25,26},{27,28},{29,30},{18,17},{2... | collective-permute-start | bytes 430088 | tf_op jit(solution)/shard_map/ppermute | solution.py:493

commit v6 on v5

--- a/solution.py
+++ b/solution.py
@@ -418,13 +418,12 @@
 
 def outer_kernel(
     slot_ref, odd_ref, inner_halo, outer_halo, stiff_ref, pull_ref, push_ref, gust_ref, pos_in,
-    vel_in, pos, vel, out_ref, coef, *, rows, far
+    vel_in, coef, pos, vel, out_ref, *, rows, far
 ):
     near = far - 2
     top = far + 2
     slot = slot_ref[0]
     sweeps = jnp.where(slot == 0, FINE + 1, 2 * FINE + 1)
-    fill_coef(coef, gust_ref, slot)
 
     def fill_halo(low, high):
         for i in range(far):
@@ -540,35 +539,33 @@
     return jax.ShapeDtypeStruct(shape, jnp.float32)
 
 
-def coef_scratch():
-    return [pltpu.VMEM((2 * FINE + 1, 3, SUBLANES, LANES), jnp.float32)]
+def coef_table():
+    return jax.ShapeDtypeStruct((2 * FINE + 1, 3, SUBLANES, LANES), jnp.float32)
 
 
 def inner_call(slot, edge, mid, stiff, pull, push, gusts, rows, far):
     return pl.pallas_call(
         functools.partial(inner_kernel, rows=rows, far=far),
-        out_shape=(state_planes(rows, far),) * 2,
+        out_shape=(state_planes(rows, far),) * 2 + (coef_table(),),
         in_specs=in_smem(1) + in_vmem(6),
-        out_specs=tuple(in_vmem(2)),
-        scratch_shapes=coef_scratch(),
+        out_specs=tuple(in_vmem(3)),
         compiler_params=pltpu.CompilerParams(vmem_limit_bytes=24 * 2**20),
         name="inner",
     )(slot, edge, mid, stiff, pull, push, gusts)
 
 
-def outer_call(slot, odd, inner, outer, stiff, pull, push, gusts, pos, vel, rows, far):
+def outer_call(slot, odd, inner, outer, stiff, pull, push, gusts, pos, vel, coef, rows, far):
     planes = state_planes(rows, far)
     out = jax.ShapeDtypeStruct((2 * rows * SUBLANES, LANES), jnp.float32)
     return pl.pallas_call(
         functools.partial(outer_kernel, rows=rows, far=far),
         out_shape=(planes, planes, out),
-        in_specs=in_smem(2) + in_vmem(8),
+        in_specs=in_smem(2) + in_vmem(9),
         out_specs=tuple(in_vmem(3)),
-        scratch_shapes=coef_scratch(),
         input_output_aliases={8: 0, 9: 1},
         compiler_params=pltpu.CompilerParams(vmem_limit_bytes=24 * 2**20),
         name="outer",
-    )(slot, odd, inner, outer, stiff, pull, push, gusts, pos, vel)[2]
+    )(slot, odd, inner, outer, stiff, pull, push, gusts, pos, vel, coef)[2]
 
 
 def two_slice_device(start_state, rigidity, inv_mass, gust_load, kl_coeff, gust_history):
@@ -644,7 +641,7 @@
     )
     inner = sent(second_edge, swap_pairs(space_count, 0))
     gusts = jnp.stack([first_edge[side], own_gusts])
-    pos, vel = inner_call(slot, edge, mid, stiff, pull, push, gusts, rows, far)
+    pos, vel, coef = inner_call(slot, edge, mid, stiff, pull, push, gusts, rows, far)
 
     blank = jnp.zeros((away, SUBLANES, LANES), jnp.float32)
     of_even = jnp.concatenate([early[:few], blank, early[few:], blank])
@@ -662,7 +659,7 @@
     pull = spread(low[wide:wide + near], pull, high[wide:wide + near])
     push = spread(low[wide + near:], push, high[wide + near:])
     out = outer_call(
-        slot, parity, inner, outer, stiff, pull, push, gusts, pos, vel, rows, far
+        slot, parity, inner, outer, stiff, pull, push, gusts, pos, vel, coef, rows, far
     )
     return from_tile_view(out, start_state.shape)
 

time: 26 us -> 26.1 us (level)
  no operation moved by 1% of the time
where the time goes in v6:
time: 26.1 us; the launch traced here: 25.9 us
  starting transfers between devices  12.9 us (49%)
  Pallas kernels  7.17 us (27%)
  waiting for transfers between devices  4.73 us (18%)
  other arithmetic  0.61 us (2%)
  between operations  0.34 us (1%)
    ppermute x5, starting transfers between devices, sent(): return lax.ppermute(block, axes, pairs)  8.31 us
    ppermute x5, waiting for transfers between devices, sent(): return lax.ppermute(block, axes, pairs)  4.72 us
    ppermute x3, starting transfers between devices, passed_along(): return lax.ppermute(block, axis, route)  4.6 us
    pallas_call x1, Pallas kernels, outer_call(): pl.pallas_call(functools.partial(outer_kernel, rows=rows, far=far), out_s...  2.36 us
    pallas_call x1, Pallas kernels, field_call(): pl.pallas_call(field_kernel, out_shape=(plane(rows),) * 3 + (jax.ShapeDty...  1.92 us
    pallas_call x1, Pallas kernels, inner_call(): pl.pallas_call(functools.partial(inner_kernel, rows=rows, far=far), out_s...  1.74 us
    pallas_call x1, Pallas kernels, two_slice_device(): pl.pallas_call(functools.partial(pack_kernel, rows=rows, far=far), out_sh...  1.15 us
  transfers between devices with their start and end apart: 8, of which 1 were waited for; matrix products, arithmetic and copies ran while one was open for 3% of the time, Pallas kernels for 14%

profile of v6, /device:TPU:9, one launch (start us, length us, event | category | flops | bytes accessed | tf_op | source)
XLA Modules:
  0.0 25.9 jit_solution(8070464816041994433)
XLA Ops:
  0.0 1.1 %pack.1 = (f32[35,8,128]{2,1,0:T(8,128)S(1)}, f32[34,8,128]{2,1,0:T(8,128)S(1)}, f32[60,8,128]{2,1,0:T(8,128)S(1)}) custom-call(s32[1]{0:T(128)} %bitcast.slot_ref, s32[1]{0:T(128)} %bitcast.1.odd_ref, f32[4]{0:T(128)} %gust_hbm.1, f32[1024,128]{1,0:T(8,128)} %bitcast.29), custom_call_target="tpu_custom_call" | custom-call | tf_op jit(solution)/shard_map/pack/pallas_call | solution.py:584
  1.2 2.0 %collective-permute-start.3 = (f32[35,8,128]{2,1,0:T(8,128)S(1)}, f32[35,8,128]{2,1,0:T(8,128)S(1)}, u32[]{:S(2)}, u32[]{:S(2)}) collective-permute-start(f32[35,8,128]{2,1,0:T(8,128)S(1)} %get-tuple-element.28), channel_id=1, source_target_pairs={{0,16},{1,17},{2,18},{3,19},{4,20},{5,21},{6,22},{7,23},{8,24},{9,... | collective-permute-start | bytes 430088 | tf_op jit(solution)/shard_map/ppermute | solution.py:38
  3.2 4.0 %collective-permute-start.2 = (f32[18,8,128]{2,1,0:T(8,128)S(1)}, f32[18,8,128]{2,1,0:T(8,128)S(1)}, u32[]{:S(2)}, u32[]{:S(2)}) collective-permute-start(f32[18,8,128]{2,1,0:T(8,128)S(1)} %maximum_select_fusion.1), channel_id=1, source_target_pairs={{1,2},{3,4},{5,6},{7,8},{9,10},{11,12},{13,14},{2,1},{4,3},{6,5},{... | collective-permute-start | bytes 221192 | tf_op jit(solution)/shard_map/ppermute | solution.py:492
  7.2 1.3 %collective-permute-start = (f32[34,8,128]{2,1,0:T(8,128)S(1)}, f32[34,8,128]{2,1,0:T(8,128)S(1)}, u32[]{:S(2)}, u32[]{:S(2)}) collective-permute-start(f32[34,8,128]{2,1,0:T(8,128)S(1)} %get-tuple-element.20), channel_id=1, source_target_pairs={{0,16},{1,17},{2,18},{3,19},{4,20},{5,21},{6,22},{7,23},{8,24},{9,... | collective-permute-start | bytes 417800 | tf_op jit(solution)/shard_map/ppermute | solution.py:38
  8.5 1.3 %collective-permute-start.7 = (f32[60,8,128]{2,1,0:T(8,128)S(1)}, f32[60,8,128]{2,1,0:T(8,128)S(1)}, u32[]{:S(2)}, u32[]{:S(2)}) collective-permute-start(f32[60,8,128]{2,1,0:T(8,128)S(1)} %get-tuple-element.30), channel_id=1, source_target_pairs={{0,16},{1,17},{2,18},{3,19},{4,20},{5,21},{6,22},{7,23},{8,24},{9,... | collective-permute-start | bytes 737288 | tf_op jit(solution)/shard_map/ppermute | solution.py:38
  9.9 0.1 multiply_cosine_fusion.1.across_ref
  10.0 0.1 multiply_cosine_fusion.along_ref
  10.1 1.9 %field.1 = (f32[64,8,128]{2,1,0:T(8,128)S(1)}, f32[64,8,128]{2,1,0:T(8,128)S(1)}, f32[64,8,128]{2,1,0:T(8,128)S(1)}, f32[8,128]{1,0:T(8,128)S(1)}) custom-call(f32[4,64]{1,0:T(4,128)S(1)} %multiply_cosine_fusion.1.across_ref, f32[4,8,128]{2,1,0:T(8,128)S(1)} %multiply_cosine_fusion.along_ref, f32[4,4]{1,0:T(4,128)} %kl_hbm.1, f32[4]{0:T(128)} %gust_hbm.1, ...), custom_call_target="tpu_custom_call" | custom-call | tf_op jit(solution)/shard_map/field/pallas_call | solution.py:513
  12.2 0.1 collective-permute-start.5
  12.2 0.0 collective-permute-done.2
  12.2 3.5 %collective-permute-start.6 = (f32[49,8,128]{2,1,0:T(8,128)S(1)}, f32[49,8,128]{2,1,0:T(8,128)S(1)}, u32[]{:S(2)}, u32[]{:S(2)}) collective-permute-start(f32[49,8,128]{2,1,0:T(8,128)S(1)} %get-tuple-element.40), channel_id=1, source_target_pairs={{1,2},{3,4},{5,6},{7,8},{9,10},{11,12},{13,14},{2,1},{4,3},{6,5},{... | collective-permute-start | bytes 602120 | tf_op jit(solution)/shard_map/ppermute | solution.py:492
  15.8 0.0 collective-permute-done.3
  15.8 0.0 collective-permute-done
  15.9 0.1 collective-permute-start.1
  16.0 0.7 %collective-permute-start.4 = (f32[35,8,128]{2,1,0:T(8,128)S(1)}, f32[35,8,128]{2,1,0:T(8,128)S(1)}, u32[]{:S(2)}, u32[]{:S(2)}) collective-permute-start(f32[35,8,128]{2,1,0:T(8,128)S(1)} %collective-permute-done.3), channel_id=1, source_target_pairs={{17,18},{19,20},{21,22},{23,24},{25,26},{27,28},{29,30},{18,17},{2... | collective-permute-start | bytes 430088 | tf_op jit(solution)/shard_map/ppermute | solution.py:492
  16.7 0.0 collective-permute-done.5
  16.7 4.7 %collective-permute-done.6 = f32[49,8,128]{2,1,0:T(8,128)S(1)} collective-permute-done((f32[49,8,128]{2,1,0:T(8,128)S(1)}, f32[49,8,128]{2,1,0:T(8,128)S(1)}, u32[]{:S(2)}, u32[]{:S(2)}) %collective-permute-start.6) | collective-permute-done | bytes 200736 | tf_op jit(solution)/shard_map/ppermute | solution.py:492
  21.4 0.1 broadcast_select_fusion.2
  21.6 0.1 select_maximum_fusion
  21.6 0.0 collective-permute-done.7
  21.7 1.7 %inner.1 = (f32[10,104,8,128]{3,2,1,0:T(8,128)S(1)}, f32[10,104,8,128]{3,2,1,0:T(8,128)S(1)}, f32[9,3,8,128]{3,2,1,0:T(8,128)S(1)}) custom-call(s32[1]{0:T(128)} %bitcast.slot_ref, f32[68,8,128]{2,1,0:T(8,128)S(1)} %pad_maximum_fusion.edge_ref, f32[60,8,128]{2,1,0:T(8,128)S(1)} %broadcast_select_fusion.mid_ref, ...), custom_call_target="tpu_custom_call" | custom-call | tf_op jit(solution)/shard_map/inner/pallas_call | solution.py:547
  23.4 0.0 collective-permute-done.4
  23.5 0.0 collective-permute-done.1.inner_halo
  23.5 2.4 %outer.1 = (f32[10,104,8,128]{3,2,1,0:T(8,128)S(1)}, f32[10,104,8,128]{3,2,1,0:T(8,128)S(1)}, f32[1024,128]{1,0:T(8,128)}) custom-call(s32[1]{0:T(128)} %bitcast.slot_ref, s32[1]{0:T(128)} %bitcast.1.odd_ref, f32[34,8,128]{2,1,0:T(8,128)S(1)} %collective-permute-done.1.inner_halo, ...), custom_call_target="tpu_custom_call", output_to_operand_aliasing={{0}: (8, {}), {1}: (9, {})} | custom-call | tf_op jit(solution)/shard_map/outer/pallas_call | solution.py:560
  (26 shorter events, 0.4 us)
Async XLA Ops:
  1.2 14.6 %collective-permute-start.3 = (f32[35,8,128]{2,1,0:T(8,128)S(1)}, f32[35,8,128]{2,1,0:T(8,128)S(1)}, u32[]{:S(2)}, u32[]{:S(2)}) collective-permute-start(f32[35,8,128]{2,1,0:T(8,128)S(1)} %get-tuple-element.28), channel_id=1, source_target_pairs={{0,16},{1,17},{2,18},{3,19},{4,20},{5,21},{6,22},{7,23},{8,24},{9,... | collective-permute-start | bytes 430088 | tf_op jit(solution)/shard_map/ppermute | solution.py:38
  3.2 9.0 %collective-permute-start.2 = (f32[18,8,128]{2,1,0:T(8,128)S(1)}, f32[18,8,128]{2,1,0:T(8,128)S(1)}, u32[]{:S(2)}, u32[]{:S(2)}) collective-permute-start(f32[18,8,128]{2,1,0:T(8,128)S(1)} %maximum_select_fusion.1), channel_id=1, source_target_pairs={{1,2},{3,4},{5,6},{7,8},{9,10},{11,12},{13,14},{2,1},{4,3},{6,5},{... | collective-permute-start | bytes 221192 | tf_op jit(solution)/shard_map/ppermute | solution.py:492
  7.2 8.6 %collective-permute-start = (f32[34,8,128]{2,1,0:T(8,128)S(1)}, f32[34,8,128]{2,1,0:T(8,128)S(1)}, u32[]{:S(2)}, u32[]{:S(2)}) collective-permute-start(f32[34,8,128]{2,1,0:T(8,128)S(1)} %get-tuple-element.20), channel_id=1, source_target_pairs={{0,16},{1,17},{2,18},{3,19},{4,20},{5,21},{6,22},{7,23},{8,24},{9,... | collective-permute-start | bytes 417800 | tf_op jit(solution)/shard_map/ppermute | solution.py:38
  8.5 13.1 %collective-permute-start.7 = (f32[60,8,128]{2,1,0:T(8,128)S(1)}, f32[60,8,128]{2,1,0:T(8,128)S(1)}, u32[]{:S(2)}, u32[]{:S(2)}) collective-permute-start(f32[60,8,128]{2,1,0:T(8,128)S(1)} %get-tuple-element.30), channel_id=1, source_target_pairs={{0,16},{1,17},{2,18},{3,19},{4,20},{5,21},{6,22},{7,23},{8,24},{9,... | collective-permute-start | bytes 737288 | tf_op jit(solution)/shard_map/ppermute | solution.py:38
  12.2 4.6 %collective-permute-start.5 = (f32[49,8,128]{2,1,0:T(8,128)S(1)}, f32[49,8,128]{2,1,0:T(8,128)S(1)}, u32[]{:S(2)}, u32[]{:S(2)}) collective-permute-start(f32[49,8,128]{2,1,0:T(8,128)S(1)} %get-tuple-element.39), channel_id=1, source_target_pairs={{0,1},{2,3},{4,5},{6,7},{8,9},{10,11},{12,13},{14,15},{1,0},{3,2},... | collective-permute-start | bytes 602120 | tf_op jit(solution)/shard_map/ppermute | solution.py:492
  12.2 9.2 %collective-permute-start.6 = (f32[49,8,128]{2,1,0:T(8,128)S(1)}, f32[49,8,128]{2,1,0:T(8,128)S(1)}, u32[]{:S(2)}, u32[]{:S(2)}) collective-permute-start(f32[49,8,128]{2,1,0:T(8,128)S(1)} %get-tuple-element.40), channel_id=1, source_target_pairs={{1,2},{3,4},{5,6},{7,8},{9,10},{11,12},{13,14},{2,1},{4,3},{6,5},{... | collective-permute-start | bytes 602120 | tf_op jit(solution)/shard_map/ppermute | solution.py:492
  15.9 7.6 %collective-permute-start.1 = (f32[34,8,128]{2,1,0:T(8,128)S(1)}, f32[34,8,128]{2,1,0:T(8,128)S(1)}, u32[]{:S(2)}, u32[]{:S(2)}) collective-permute-start(f32[34,8,128]{2,1,0:T(8,128)S(1)} %get-tuple-element.36), channel_id=1, source_target_pairs={{0,1},{2,3},{4,5},{6,7},{8,9},{10,11},{12,13},{14,15},{1,0},{3,2},... | collective-permute-start | bytes 417800 | tf_op jit(solution)/shard_map/ppermute | solution.py:492
  16.0 7.5 %collective-permute-start.4 = (f32[35,8,128]{2,1,0:T(8,128)S(1)}, f32[35,8,128]{2,1,0:T(8,128)S(1)}, u32[]{:S(2)}, u32[]{:S(2)}) collective-permute-start(f32[35,8,128]{2,1,0:T(8,128)S(1)} %collective-permute-done.3), channel_id=1, source_target_pairs={{17,18},{19,20},{21,22},{23,24},{25,26},{27,28},{29,30},{18,17},{2... | collective-permute-start | bytes 430088 | tf_op jit(solution)/shard_map/ppermute | solution.py:492
